TPU v7x, 512 devices: a whole 4x4x16 slice. The times are simulated.
512 devices in a mesh: emb: 64 (over z, x), bal: 8 (over y, core).
Axes of the slice: x: 4, y: 4, z: 16, core: 2. Of those that a mesh axis runs over, the one named last changes fastest.
Arguments:
- item_ids: int32 [8, 16384, 16], P('bal'), may hold values from 0 to 1023
- seq_lengths: int32 [8, 64, 2], P(None, 'emb'), may hold values from 1 to 128, as said below
- surplus_slot: int32 [8, 64], P(None, 'emb'), may hold values from 0 to 1
- helper_map: int32 [8, 64], P(None, 'emb'), may hold values from 0 to 7, as said below
- embed_tables: bfloat16 [64, 1024, 128], P('emb'), may hold values from -1.5 to 1.5
- weight_in: bfloat16 [512, 2048], P('bal'), may hold values from -0.25 to 0.25
- weight_out: bfloat16 [512, 512], P('bal'), may hold values from -0.25 to 0.25
- cotangent: bfloat16 [8, 16384, 512], P('bal', 'emb'), may hold values from -6 to 6
Outputs:
- layer_out: bfloat16 [8, 16384, 512], P('bal', 'emb')
- table_grad: float32 [64, 1024, 128], P('emb', 'bal')
- grad_in: float32 [512, 2048], P('bal')
- grad_out: float32 [512, 512], P('bal')
Inputs may be any that keep to these rules, and one draw needn't show every extreme that they name: `seq_lengths`: some slot has 128 live events. Each column helper_map[:, e] is a permutation of the bal indices.
All inputs are finite; a program needn't handle non-finite values.
Results may differ from a plain program's by a relative error of at most 0.014.
Values may be sent and summed in bfloat16 or wider, within the bound.
A program may use at most 64 MiB of HBM per device.

v0:
```python
import jax
import jax.numpy as jnp
from jax import lax
from jax.sharding import PartitionSpec as P

D = 512
HEADS = 8
COLS = 128
DISTINCT = 1024
SLOT = 128
NSEQ = 2


EPS = 1e-05


def silu_grad(argument):
    logistic = jax.nn.sigmoid(argument)
    return logistic * (1.0 + argument * (1.0 - logistic))


def seq_mask(lengths, row_count, slot_rows):
    position = jnp.arange(row_count, dtype=jnp.int32)
    slot_of = position // slot_rows
    within = position - slot_of * slot_rows
    slot_ids = jnp.arange(lengths.shape[0], dtype=jnp.int32)
    row_length = jnp.sum(
        jnp.where(slot_of[:, None] == slot_ids[None, :], lengths[None, :], 0), axis=1
    )
    same_slot = slot_of[:, None] == slot_of[None, :]
    causal = position[None, :] <= position[:, None]
    live = within[:, None] < row_length[:, None]
    return jnp.where(same_slot & causal & live, 1.0, 0.0).astype(jnp.float32)


def normalize(values):
    average = jnp.mean(values, axis=1, keepdims=True)
    centred = values - average
    inverse = lax.rsqrt(jnp.mean(centred * centred, axis=1, keepdims=True) + EPS)
    return (centred * inverse, inverse)


def norm_back(incoming, normed, inverse):
    first = jnp.mean(incoming, axis=1, keepdims=True)
    second = jnp.mean(incoming * normed, axis=1, keepdims=True)
    return inverse * (incoming - first - normed * second)


def head_slices(heads_input, head_index, head_width, model_width):
    head_values = lax.dynamic_slice_in_dim(heads_input, head_index * head_width, head_width, 1)
    head_query = lax.dynamic_slice_in_dim(
        heads_input, model_width + head_index * head_width, head_width, 1
    )
    head_keys = lax.dynamic_slice_in_dim(
        heads_input, 2 * model_width + head_index * head_width, head_width, 1
    )
    return (head_values, head_query, head_keys)


def head_forward(heads_input, allowed, head_index, head_width, model_width, seq_bound):
    head_values, head_query, head_keys = head_slices(
        heads_input, head_index, head_width, model_width
    )
    scores = jnp.dot(head_query, head_keys.T, preferred_element_type=jnp.float32) * head_width ** (
        -0.5
    )
    silu_weights = (jax.nn.silu(scores) * allowed / seq_bound).astype(jnp.bfloat16)
    return jnp.dot(silu_weights, head_values, preferred_element_type=jnp.float32)


def head_backward(
    heads_input, allowed, grad_attended, head_index, head_width, model_width, seq_bound
):
    head_values, head_query, head_keys = head_slices(
        heads_input, head_index, head_width, model_width
    )
    score_scale = head_width ** (-0.5)
    scores = jnp.dot(head_query, head_keys.T, preferred_element_type=jnp.float32) * score_scale
    silu_weights = (jax.nn.silu(scores) * allowed / seq_bound).astype(jnp.bfloat16)
    grad_head = lax.dynamic_slice_in_dim(grad_attended, head_index * head_width, head_width, 1)
    grad_weights = jnp.dot(grad_head, head_values.T, preferred_element_type=jnp.float32)
    grad_values = jnp.dot(silu_weights.T, grad_head, preferred_element_type=jnp.float32)
    grad_scores = (grad_weights * allowed / seq_bound * silu_grad(scores)).astype(jnp.bfloat16)
    grad_query = jnp.dot(grad_scores, head_keys, preferred_element_type=jnp.float32) * score_scale
    grad_keys = jnp.dot(grad_scores.T, head_query, preferred_element_type=jnp.float32) * score_scale
    return (grad_values, grad_query, grad_keys)


def join_heads(stacked):
    head_count, row_count, head_width = stacked.shape
    return jnp.transpose(stacked, (1, 0, 2)).reshape(row_count, head_count * head_width)


def layer_forward(inputs, lengths, weight_in, weight_out, head_count, slot_rows):
    row_count, model_width = inputs.shape
    head_width = model_width // head_count
    allowed = seq_mask(lengths, row_count, slot_rows)
    normed_in, in_inverse = normalize(inputs.astype(jnp.float32))
    normed_half = normed_in.astype(jnp.bfloat16)
    projected = jnp.dot(normed_half, weight_in, preferred_element_type=jnp.float32)
    activated = jax.nn.silu(projected)
    gate_rows = activated[:, :model_width]
    heads_input = activated[:, model_width:].astype(jnp.bfloat16)
    head_ids = jnp.arange(head_count, dtype=jnp.int32)
    attended = lax.map(
        lambda head_index: head_forward(
            heads_input, allowed, head_index, head_width, model_width, slot_rows
        ),
        head_ids,
    )
    normed_out, out_inverse = normalize(join_heads(attended))
    mixed_rows = (normed_out * gate_rows).astype(jnp.bfloat16)
    forward_out = (
        inputs.astype(jnp.float32)
        + jnp.dot(mixed_rows, weight_out, preferred_element_type=jnp.float32)
    ).astype(jnp.bfloat16)
    stored = (
        allowed,
        normed_in,
        in_inverse,
        normed_half,
        projected,
        gate_rows,
        heads_input,
        normed_out,
        out_inverse,
        mixed_rows,
    )
    return (forward_out, stored)


def layer_backward(stored, cotangent, weight_in, weight_out, head_count, slot_rows):
    (
        allowed,
        normed_in,
        in_inverse,
        normed_half,
        projected,
        gate_rows,
        heads_input,
        normed_out,
        out_inverse,
        mixed_rows,
    ) = stored
    row_count, model_width = normed_in.shape
    head_width = model_width // head_count
    partial_out = jnp.dot(mixed_rows.T, cotangent, preferred_element_type=jnp.float32)
    grad_mixed = jnp.dot(cotangent, weight_out.T, preferred_element_type=jnp.float32)
    grad_gate = grad_mixed * normed_out
    grad_attended = norm_back(grad_mixed * gate_rows, normed_out, out_inverse).astype(jnp.bfloat16)
    head_ids = jnp.arange(head_count, dtype=jnp.int32)
    head_grads = lax.map(
        lambda head_index: head_backward(
            heads_input, allowed, grad_attended, head_index, head_width, model_width, slot_rows
        ),
        head_ids,
    )
    grad_heads = jnp.concatenate(
        [join_heads(head_grads[0]), join_heads(head_grads[1]), join_heads(head_grads[2])], axis=1
    )
    grad_projected = (
        jnp.concatenate([grad_gate, grad_heads], axis=1) * silu_grad(projected)
    ).astype(jnp.bfloat16)
    partial_in = jnp.dot(normed_half.T, grad_projected, preferred_element_type=jnp.float32)
    grad_normed = jnp.dot(grad_projected, weight_in.T, preferred_element_type=jnp.float32)
    grad_rows = (
        cotangent.astype(jnp.float32) + norm_back(grad_normed, normed_in, in_inverse)
    ).astype(jnp.bfloat16)
    return (grad_rows, partial_in, partial_out)


def on_device(
    item_ids, seq_lengths, surplus_slot, helper_map, embed_tables, weight_in, weight_out, cotangent
):
    bal_index = lax.axis_index("bal")
    emb_index = lax.axis_index("emb")
    bal_count = lax.axis_size("bal")
    emb_count = lax.axis_size("emb")
    table_count = item_ids.shape[2]
    group_count = D // COLS
    table_pick = emb_index // group_count
    table_ids = lax.dynamic_index_in_dim(item_ids[0], table_pick, 1, keepdims=False)
    looked = embed_tables[0][table_ids]
    pieces = lax.all_to_all(looked, "emb", split_axis=0, concat_axis=1, tiled=True)
    row_count = pieces.shape[0]
    embedded = jnp.sum(pieces.reshape(row_count, table_count, D), axis=1, dtype=jnp.float32).astype(
        jnp.bfloat16
    )
    own_slots = embedded.reshape(NSEQ, SLOT, D)
    surplus_col = surplus_slot[:, 0]
    helper_col = helper_map[:, 0]
    length_col = seq_lengths[:, 0, :]
    bal_ids = jnp.arange(bal_count, dtype=jnp.int32)
    slot_ids = jnp.arange(NSEQ, dtype=jnp.int32)
    my_slot = lax.dynamic_index_in_dim(surplus_col, bal_index, 0, keepdims=False)
    leaving = lax.dynamic_index_in_dim(own_slots, my_slot, 0, keepdims=True)
    arrived_all = lax.all_gather(leaving, "bal", axis=0, tiled=True)
    source = jnp.sum(jnp.where(helper_col == bal_index, bal_ids, 0))
    arrived = lax.dynamic_index_in_dim(arrived_all, source, 0, keepdims=True)
    replaced = slot_ids == my_slot
    proc_rows = jnp.where(replaced[:, None, None], arrived, own_slots).reshape(row_count, D)
    own_lengths = lax.dynamic_index_in_dim(length_col, bal_index, 0, keepdims=False)
    source_lengths = lax.dynamic_index_in_dim(length_col, source, 0, keepdims=False)
    source_slot = lax.dynamic_index_in_dim(surplus_col, source, 0, keepdims=False)
    moved_length = jnp.sum(jnp.where(slot_ids == source_slot, source_lengths, 0))
    proc_lengths = jnp.where(replaced, moved_length, own_lengths)
    full_in, full_out = (
        lax.all_gather(weight_in, "bal", axis=0, tiled=True),
        lax.all_gather(weight_out, "bal", axis=0, tiled=True),
    )
    forward_out, stored = layer_forward(proc_rows, proc_lengths, full_in, full_out, HEADS, SLOT)
    back_in, back_out = (full_in, full_out)
    grad_rows, partial_in, partial_out = layer_backward(
        stored, cotangent[0], back_in, back_out, HEADS, SLOT
    )
    grad_slots = grad_rows.reshape(NSEQ, SLOT, D)
    outgoing = lax.dynamic_index_in_dim(grad_slots, my_slot, 0, keepdims=True)
    returned_all = lax.all_gather(outgoing, "bal", axis=0, tiled=True)
    helper = lax.dynamic_index_in_dim(helper_col, bal_index, 0, keepdims=False)
    came_back = lax.dynamic_index_in_dim(returned_all, helper, 0, keepdims=True)
    anchor_grads = jnp.where(replaced[:, None, None], came_back, grad_slots).reshape(row_count, D)
    copies = jnp.tile(anchor_grads, (1, table_count))
    table_rows = lax.all_to_all(copies, "emb", split_axis=1, concat_axis=0, tiled=True)
    table_part = (
        jnp.zeros((DISTINCT, COLS), jnp.float32).at[table_ids].add(table_rows.astype(jnp.float32))
    )
    table_sum = lax.psum_scatter(
        table_part.astype(jnp.bfloat16), "bal", scatter_dimension=0, tiled=True
    ).astype(jnp.float32)
    table_scale = (DISTINCT / (bal_count * item_ids.shape[1])) ** 0.5
    owned_in, owned_out = (
        lax.psum_scatter(
            partial_in.astype(jnp.bfloat16), "bal", scatter_dimension=0, tiled=True
        ).astype(jnp.float32),
        lax.psum_scatter(
            partial_out.astype(jnp.bfloat16), "bal", scatter_dimension=0, tiled=True
        ).astype(jnp.float32),
    )
    total_in, total_out = lax.psum((owned_in, owned_out), "emb")
    events = row_count * emb_count * bal_count
    grad_scale = events ** (-0.5)
    return (
        forward_out[None],
        (table_sum * table_scale)[None],
        total_in * grad_scale,
        total_out * grad_scale,
    )


def solution(mesh):
    placed = (
        P("bal", None, None),
        P(None, "emb", None),
        P(None, "emb"),
        P(None, "emb"),
        P("emb", None, None),
        P("bal", None),
        P("bal", None),
        P("bal", "emb", None),
    )
    return jax.shard_map(
        on_device,
        mesh=mesh,
        in_specs=placed,
        out_specs=(P("bal", "emb", None), P("emb", "bal", None), P("bal", None), P("bal", None)),
        check_vma=False,
    )
```

profile of v0, /device:TPU:6, one launch (start us, length us, event | category | flops | bytes accessed | tf_op | source)
XLA Modules:
  0.0 1064.1 jit_solution(4333655508343074322)
XLA Ops:
  7.2 1.2 compare_select_fusion
  8.4 57.4 %gather_fusion = bf16[16384,128]{1,0:T(8,128)(2,1)} fusion(bf16[1024,128]{1,0:T(8,128)(2,1)S(1)} %bitcast.105, s32[16384]{0:T(1024)S(1)} %broadcast_clamp_fusion), kind=kCustom, calls=%fused_computation | custom fusion | bytes 8454144 | tf_op jit(solution)/shard_map/gather | solution.py:183
  65.8 6.4 copy.38
  72.2 18.9 %all-to-all-start = ((bf16[64,256,128]{1,2,0:T(8,128)(2,1)}), bf16[64,256,128]{1,2,0:T(8,128)(2,1)}, u32[]{:S(2)}, u32[]{:S(2)}) async-start(bf16[64,256,128]{1,2,0:T(8,128)(2,1)} %copy.38), calls=%async_computation | async-start | bytes 8388608 | tf_op jit(solution)/shard_map/all_to_all | solution.py:184
  96.3 184.7 %all-to-all-done = bf16[64,256,128]{1,2,0:T(8,128)(2,1)} async-done(((bf16[64,256,128]{1,2,0:T(8,128)(2,1)}), bf16[64,256,128]{1,2,0:T(8,128)(2,1)}, u32[]{:S(2)}, u32[]{:S(2)}) %all-to-all-start) | async-done | bytes 4194336 | tf_op jit(solution)/shard_map/all_to_all | solution.py:184
  281.0 2.9 reduce_sum.111
  286.5 1.3 fusion.89
  287.8 1.3 broadcast_select_fusion
  289.2 14.2 %all_gather.14 = bf16[512,512]{1,0:T(8,128)(2,1)S(1)} all-gather(bf16[64,512]{1,0:T(8,128)(2,1)S(1)} %copy-done.4), channel_id=1, replica_groups=mesh['emb'=64,'bal'=8] {'bal'}, dimensions={0}, use_global_device_ids=true | all-gather | bytes 589824 | tf_op jit(solution)/shard_map/all_gather | solution.py:209
  303.4 4.2 all-gather.4.cloned.1.call-done
  307.7 0.9 dynamic-slice_bitcast_fusion.1
  309.0 33.8 %all-gather.6.cloned.1.call-done = bf16[512,2048]{1,0:T(8,128)(2,1)} async-done(((bf16[64,2048]{1,0:T(8,128)(2,1)}), bf16[512,2048]{1,0:T(8,128)(2,1)}) %all-gather.6.cloned.1.call-update) | async-done | bytes 2097168 | tf_op jit(solution)/shard_map/all_gather | solution.py:208
  342.9 3.7 fusion.64
  346.6 1.2 copy-done.3
  347.9 13.9 %while.30 = (s32[]{:T(128)}, f32[8,256,64]{1,2,0:T(8,128)S(1)}, s32[8]{0:T(128)S(1)}, bf16[256,1536]{1,0:T(8,128)(2,1)S(1)}, s32[256]{0:T(256)S(1)}, /*index=5*/...) while((s32[]{:T(128)}, f32[8,256,64]{1,2,0:T(8,128)S(1)}, ...), condition=%wide.region_7.8_spmd.clone, body=%wide.region_6.7_spmd.clone.sunk | while | flops 17629196 | bytes 265011 | solution.py:105
  362.8 1.5 fusion.94
  364.3 2.1 multiply_convert_fusion
  368.1 31.5 %while.31 = (s32[]{:T(128)}, f32[8,256,64]{1,2,0:T(8,128)}, f32[8,256,64]{1,2,0:T(8,128)}, f32[8,256,64]{1,2,0:T(8,128)S(1)}, s32[8]{0:T(128)S(1)}, /*index=5*/b...) while((s32[]{:T(128)}, f32[8,256,64]{1,2,0:T(8,128)}, ...), condition=%wide.region_13.14_spmd.clone, body=%wide.region_12.13_spmd.clone.sunk | while | flops 43876364 | bytes 1840496 | solution.py:152
  370.0 0.9 fusion.138
  373.9 0.9 fusion.138
  375.1 0.9 fusion.140
  377.9 0.9 fusion.138
  381.8 0.9 fusion.138
  383.0 0.9 fusion.140
  385.7 0.9 fusion.138
  389.7 0.9 fusion.138
  393.6 0.9 fusion.138
  394.8 0.9 fusion.140
  397.6 0.9 fusion.138
  399.7 1.0 copy.44
  400.7 2.1 copy.42
  402.7 1.0 copy.43
  403.7 3.1 fusion.63
  410.4 29.8 %all-gather.8.cloned.1.call-done = bf16[8,128,512]{2,1,0:T(8,128)(2,1)} async-done(((bf16[1,128,512]{2,1,0:T(8,128)(2,1)}), bf16[8,128,512]{2,1,0:T(8,128)(2,1)}) %all-gather.8.cloned.1.call-update) | async-done | bytes 1048592 | tf_op jit(solution)/shard_map/all_gather | solution.py:218
  440.2 0.9 dynamic-slice_bitcast_fusion
  441.4 2.3 tile.2
  443.7 15.9 %all-to-all-start.1 = ((bf16[256,64,128]{0,2,1:T(8,128)(2,1)}), bf16[256,64,128]{0,2,1:T(8,128)(2,1)}, u32[]{:S(2)}, u32[]{:S(2)}) async-start(bf16[256,64,128]{0,2,1:T(8,128)(2,1)} %bitcast.107), calls=%async_computation.1 | async-start | bytes 8388608 | tf_op jit(solution)/shard_map/all_to_all | solution.py:223
  459.7 1.1 convolution_convert_fusion.1
  461.0 2.2 convolution_convert_fusion
  463.3 1.0 fusion.66
  464.3 38.5 %reduce-scatter.8.cloned.1.call-done = bf16[64,512]{1,0:T(8,128)(2,1)} async-done(((bf16[512,512]{1,0:T(8,128)(2,1)}), bf16[64,512]{1,0:T(8,128)(2,1)}) %reduce-scatter.8.cloned.1.call-update) | async-done | bytes 65552 | tf_op jit(solution)/shard_map/reduce_scatter | solution.py:235
  502.8 44.2 %reduce-scatter.6.cloned.1.call-done = bf16[64,2048]{1,0:T(8,128)(2,1)} async-done(((bf16[512,2048]{1,0:T(8,128)(2,1)}), bf16[64,2048]{1,0:T(8,128)(2,1)}) %reduce-scatter.6.cloned.1.call-update) | async-done | bytes 262160 | tf_op jit(solution)/shard_map/reduce_scatter | solution.py:232
  547.0 358.7 %all-reduce.2 = (f32[64,2048]{1,0:T(8,128)S(1)}, f32[64,512]{1,0:T(8,128)S(1)}) all-reduce(bf16[64,2048]{1,0:T(8,128)(2,1)} %reduce-scatter.6.cloned.1.call-done, bf16[64,512]{1,0:T(8,128)(2,1)} %reduce-scatter.8.cloned.1.call-done), channel_id=1, replica_groups=mesh['emb'=64,'bal'=8] {'emb'}, use_global_device_ids=true, to_apply=%region_19.20 | all-reduce | flops 163840 | bytes 983040 | tf_op jit(solution)/shard_map/psum | solution.py:239
  905.8 6.5 convert_bitcast_fusion
  912.3 9.0 copy.46
  921.3 87.7 %scatter_custom_fusion = f32[1024,128]{1,0:T(8,128)S(1)} fusion(s32[16384]{0:T(1024)S(1)} %bitcast.116, f32[16384,128]{1,0:T(8,128)} %bitcast.109, f32[]{:T(128)} %constant.235.clone.1), kind=kCustom, calls=%fused_computation.110 | custom fusion | flops 2097152 | bytes 524800 | tf_op jit(solution)/shard_map/scatter-add | solution.py:225
  1011.3 44.5 %reduce-scatter.4.cloned.1.call-done = bf16[128,128]{1,0:T(8,128)(2,1)} async-done(((bf16[1024,128]{1,0:T(8,128)(2,1)}), bf16[128,128]{1,0:T(8,128)(2,1)}) %reduce-scatter.4.cloned.1.call-update) | async-done | bytes 32784 | tf_op jit(solution)/shard_map/reduce_scatter | solution.py:227
  1055.9 1.4 multiply_bitcast_fusion
  (122 shorter events, 36.2 us)
Async XLA Ops:
  7.2 1.2 copy-start
  72.2 19.0 %copy-start.7 = (s32[8,1]{0,1:T(1,128)S(1)}, s32[8,1]{0,1:T(1,128)}, u32[]{:S(2)}) copy-start(s32[8,1]{0,1:T(1,128)} %param.15) | copy-start | bytes 100
  72.2 21.6 %copy-start.6 = (s32[8,1]{0,1:T(1,128)S(1)}, s32[8,1]{0,1:T(1,128)}, u32[]{:S(2)}) copy-start(s32[8,1]{0,1:T(1,128)} %param.14) | copy-start | bytes 100
  72.2 208.9 %all-to-all-start = ((bf16[64,256,128]{1,2,0:T(8,128)(2,1)}), bf16[64,256,128]{1,2,0:T(8,128)(2,1)}, u32[]{:S(2)}, u32[]{:S(2)}) async-start(bf16[64,256,128]{1,2,0:T(8,128)(2,1)} %copy.38), calls=%async_computation | async-start | bytes 8388608 | tf_op jit(solution)/shard_map/all_to_all | solution.py:184
  91.1 216.6 %all-gather.4.cloned.1.call-start = ((), (), s32[]{:S(2)}) async-start(), calls=%async_computation.5 | async-start | bytes 1179648 | tf_op jit(solution)/shard_map/all_gather | solution.py:197
  281.0 4.5 copy-start.5
  281.0 8.2 copy-start.4
  284.8 58.1 %all-gather.6.cloned.1.call-start = ((), (), s32[]{:S(2)}) async-start(), calls=%async_computation.6 | async-start | bytes 2359296 | tf_op jit(solution)/shard_map/all_gather | solution.py:208
  285.5 154.7 %all-gather.8.cloned.1.call-start = ((), (), s32[]{:S(2)}) async-start(), calls=%async_computation.7 | async-start | bytes 1179648 | tf_op jit(solution)/shard_map/all_gather | solution.py:218
  346.5 1.3 copy-start.3
  361.8 1.0 copy-start.1
  399.7 3.1 copy-start.2
  403.7 3.1 copy-start.8
  443.7 462.1 %all-to-all-start.1 = ((bf16[256,64,128]{0,2,1:T(8,128)(2,1)}), bf16[256,64,128]{0,2,1:T(8,128)(2,1)}, u32[]{:S(2)}, u32[]{:S(2)}) async-start(bf16[256,64,128]{0,2,1:T(8,128)(2,1)} %bitcast.107), calls=%async_computation.1 | async-start | bytes 8388608 | tf_op jit(solution)/shard_map/all_to_all | solution.py:223
  459.6 43.2 %reduce-scatter.8.cloned.1.call-start = ((), (), s32[]{:S(2)}) async-start(), calls=%async_computation.10 | async-start | bytes 589824 | tf_op jit(solution)/shard_map/reduce_scatter | solution.py:235
  460.8 86.2 %reduce-scatter.6.cloned.1.call-start = ((), (), s32[]{:S(2)}) async-start(), calls=%async_computation.9 | async-start | bytes 2359296 | tf_op jit(solution)/shard_map/reduce_scatter | solution.py:232
  463.3 592.6 %reduce-scatter.4.cloned.1.call-start = ((), (), s32[]{:S(2)}) async-start(), calls=%async_computation.8 | async-start | bytes 294912 | tf_op jit(solution)/shard_map/reduce_scatter | solution.py:227
Sparse Core Ops, SparseCore 0:
  284.9 22.7 all-gather.3
  309.8 33.0 all-gather.5
  408.8 31.3 all-gather.7
  463.5 39.2 reduce-scatter.7
  505.5 41.4 reduce-scatter.5
  1009.9 45.8 reduce-scatter.3
where the time goes:
time: 1070 us; the launch traced here: 1060 us
  waiting for transfers between devices  381 us (36%)
  blocking collectives  373 us (35%)
  other arithmetic  112 us (10%)
  local copies, waits for them, and re-layouts  96.7 us (9%)
  matrix products  35.4 us (3%)
  starting transfers between devices  35.2 us (3%)
  between operations  20 us (2%)
  loops' own time  11.1 us (1%)
    psum x1, blocking collectives, on_device(): total_in, total_out = lax.psum((owned_in, owned_out), 'emb')  359 us
    all_to_all x1, waiting for transfers between devices, on_device(): lax.all_to_all(looked, 'emb', split_axis=0, concat_axis=1, tiled=True)  185 us
    scatter-add x1, other arithmetic, on_device(): jnp.zeros((DISTINCT, COLS), jnp.float32).at[table_ids]  87.7 us
    gather x1, local copies, waits for them, and re-layouts, on_device(): looked = embed_tables[0][table_ids]  57.4 us
    reduce_scatter x1, waiting for transfers between devices, on_device(): lax.psum_scatter(table_part.astype(jnp.bfloat16), 'bal', scatter_dimensio...  44.5 us
    reduce_scatter x1, waiting for transfers between devices, on_device(): lax.psum_scatter(partial_in.astype(jnp.bfloat16), 'bal', scatter_dimensio...  44.2 us
    reduce_scatter x1, waiting for transfers between devices, on_device(): lax.psum_scatter(partial_out.astype(jnp.bfloat16), 'bal', scatter_dimensi...  38.5 us
    all_gather x1, waiting for transfers between devices, on_device(): lax.all_gather(weight_in, 'bal', axis=0, tiled=True)  33.8 us
  transfers between devices with their start and end apart: 8, of which 7 were waited for; matrix products, arithmetic and copies ran while one was open for 1% of the time, Pallas kernels for 0%

commit v1 on v0

v1 whole, which is shorter than its diff:
```python
import functools

import jax
import jax.numpy as jnp
from jax import lax
from jax.experimental import pallas as pl
from jax.experimental.pallas import tpu as pltpu
from jax.sharding import PartitionSpec as P

D = 512
HEADS = 8
COLS = 128
DISTINCT = 1024
SLOT = 128
NSEQ = 2
TABLES = 16
NZ = 16
NX = 4
NY = 4
NB = 8
EPS = 1e-05
BF = jnp.bfloat16
F32 = jnp.float32
VMEM_LIMIT = 64000 * 1024


def place():
    emb = lax.axis_index("emb")
    bal = lax.axis_index("bal")
    return emb // NX, emb % NX, bal // 2, bal % 2


def at(z, x, y, k):
    return {"emb": z * NX + x, "bal": y * 2 + k}


def rcopy(src, dst, send, recv, device):
    return pltpu.make_async_remote_copy(
        src_ref=src,
        dst_ref=dst,
        send_sem=send,
        recv_sem=recv,
        device_id=device,
        device_id_type=pl.DeviceIdType.MESH,
    )


def greet(devices):
    barrier = pltpu.get_barrier_semaphore()
    for device in devices:
        pl.semaphore_signal(barrier, inc=1, device_id=device, device_id_type=pl.DeviceIdType.MESH)
    pl.semaphore_wait(barrier, len(devices))


VM = pl.BlockSpec(memory_space=pltpu.VMEM)
ANY = pl.BlockSpec(memory_space=pl.ANY)
DMA = pltpu.SemaphoreType.DMA


Z_SLICES = [(d, s) for s in range(1, 9) for d in (-1, 1) if d < 0 or s < 8]
Z_INDEX = {pair: i for i, pair in enumerate(Z_SLICES)}


def gather_kernel(
    tab, win, wout, ids, meta, tabs, wfi, wfo, idall, metall,
    zs, zr, ys, yr, cs, cr, ws, wr, os_, or_, is_, ir, ms, mr, loc,
):
    z, x, y, k = place()
    right, left = at((z + 1) % NZ, x, y, k), at((z + NZ - 1) % NZ, x, y, k)
    yp, ym, y2 = (y + 1) % NY, (y + 3) % NY, (y + 2) % NY
    up, down = at(z, x, yp, k), at(z, x, ym, k)
    xp, xm, x2 = (x + 1) % NX, (x + 3) % NX, (x + 2) % NX
    east, west, far = at(z, xp, y, k), at(z, xm, y, k), at(z, x2, y, k)
    other = at(z, x, y, 1 - k)
    greet([right, left, up, down, east, west, far, other])

    sent = []

    def go(src, dst, send, recv, device):
        copy = rcopy(src, dst, send, recv, device)
        copy.start()
        sent.append(copy)

    def came(dst, send, recv, device):
        rcopy(dst, dst, send, recv, device).wait_recv()

    local = [
        pltpu.make_async_copy(tab, tabs.at[z], loc.at[0]),
        pltpu.make_async_copy(win.at[x], wfi.at[y, k, x], loc.at[1]),
        pltpu.make_async_copy(wout.at[x], wfo.at[y, k, x], loc.at[2]),
        pltpu.make_async_copy(ids, idall.at[y, k], loc.at[3]),
        pltpu.make_async_copy(meta, metall.at[x], loc.at[4]),
    ]
    go(tab.at[y, k], tabs.at[z, y, k], zs.at[0], zr.at[0], right)
    go(tab.at[y, k], tabs.at[z, y, k], zs.at[1], zr.at[1], left)
    for copy in local:
        copy.start()
    for i, (peer, dev) in enumerate(((xp, east), (xm, west), (x2, far))):
        go(meta, metall.at[x], ms.at[i], mr.at[i], dev)
    go(ids, idall.at[y, k], is_.at[0], ir.at[0], up)
    go(ids, idall.at[y, k], is_.at[1], ir.at[1], down)
    go(win.at[x], wfi.at[y, k, x], ws.at[0], wr.at[0], up)
    go(win.at[x], wfi.at[y, k, x], ws.at[1], wr.at[1], down)
    go(wout.at[x], wfo.at[y, k, x], os_.at[0], or_.at[0], up)
    go(wout.at[x], wfo.at[y, k, x], os_.at[1], or_.at[1], down)

    def slot(d, s):
        return (z + d * s + NZ) % NZ

    def weights_y_relay():
        came(idall.at[ym, k], is_.at[0], ir.at[0], up)
        go(idall.at[ym, k, 0:4], idall.at[ym, k, 0:4], is_.at[2], ir.at[2], up)
        came(idall.at[yp, k], is_.at[1], ir.at[1], down)
        go(idall.at[yp, k, 4:8], idall.at[yp, k, 4:8], is_.at[3], ir.at[3], down)
        for full, s_, r_, half in ((wfi, ws, wr, 1024), (wfo, os_, or_, 256)):
            came(full.at[ym, k, x], s_.at[0], r_.at[0], up)
            part = full.at[ym, k, x, :, 0:half]
            go(part, part, s_.at[2], r_.at[2], up)
            came(full.at[yp, k, x], s_.at[1], r_.at[1], down)
            part = full.at[yp, k, x, :, half:2 * half]
            go(part, part, s_.at[3], r_.at[3], down)

    def weights_x_send():
        came(idall.at[y2, k, 0:4], is_.at[2], ir.at[2], up)
        came(idall.at[y2, k, 4:8], is_.at[3], ir.at[3], down)
        local[3].wait()
        go(idall.at[:, k], idall.at[:, k], is_.at[4], ir.at[4], other)
        local[1].wait()
        local[2].wait()
        for full, s_, r_, half in ((wfi, ws, wr, 1024), (wfo, os_, or_, 256)):
            came(full.at[y2, k, x, :, 0:half], s_.at[2], r_.at[2], up)
            came(full.at[y2, k, x, :, half:2 * half], s_.at[3], r_.at[3], down)
            go(full.at[:, k, x], full.at[:, k, x], s_.at[4], r_.at[4], east)
            go(full.at[:, k, x], full.at[:, k, x], s_.at[5], r_.at[5], west)

    def weights_x_relay():
        for full, s_, r_ in ((wfi, ws, wr), (wfo, os_, or_)):
            came(full.at[:, k, xm], s_.at[4], r_.at[4], east)
            part = full.at[0:2, k, xm]
            go(part, part, s_.at[6], r_.at[6], east)
            came(full.at[:, k, xp], s_.at[5], r_.at[5], west)
            part = full.at[2:4, k, xp]
            go(part, part, s_.at[7], r_.at[7], west)

    def weights_core():
        for full, s_, r_ in ((wfi, ws, wr), (wfo, os_, or_)):
            came(full.at[0:2, k, x2], s_.at[6], r_.at[6], east)
            came(full.at[2:4, k, x2], s_.at[7], r_.at[7], west)
            go(full.at[:, k], full.at[:, k], s_.at[8], r_.at[8], other)

    for st in range(1, 11):
        for d in (-1, 1):
            if (d, st) not in Z_INDEX:
                continue
            i, zz = Z_INDEX[(d, st)], slot(d, st)
            mine = tabs.at[zz, y, k]
            onward = right if d < 0 else left
            came(mine, zs.at[i], zr.at[i], onward)
            if (d, st + 1) in Z_INDEX:
                j = Z_INDEX[(d, st + 1)]
                go(mine, mine, zs.at[j], zr.at[j], onward)
            go(mine, mine, ys.at[i, 0], yr.at[i, 0], up)
            go(mine, mine, ys.at[i, 1], yr.at[i, 1], down)
        for d in (-1, 1):
            if (d, st - 1) not in Z_INDEX:
                continue
            i, zz = Z_INDEX[(d, st - 1)], slot(d, st - 1)
            came(tabs.at[zz, ym, k], ys.at[i, 0], yr.at[i, 0], up)
            part = tabs.at[zz, ym, k, 0:64]
            go(part, part, ys.at[i, 2], yr.at[i, 2], up)
            came(tabs.at[zz, yp, k], ys.at[i, 1], yr.at[i, 1], down)
            part = tabs.at[zz, yp, k, 64:128]
            go(part, part, ys.at[i, 3], yr.at[i, 3], down)
        for d in (-1, 1):
            if (d, st - 2) not in Z_INDEX:
                continue
            i, zz = Z_INDEX[(d, st - 2)], slot(d, st - 2)
            came(tabs.at[zz, y2, k, 0:64], ys.at[i, 2], yr.at[i, 2], up)
            came(tabs.at[zz, y2, k, 64:128], ys.at[i, 3], yr.at[i, 3], down)
            go(tabs.at[zz, :, k], tabs.at[zz, :, k], cs.at[i], cr.at[i], other)
        if st == 1:
            weights_y_relay()
        if st == 2:
            weights_x_send()
        if st == 5:
            weights_x_relay()
        if st == 8:
            weights_core()

    for i, peer in enumerate((xm, xp, x2)):
        came(metall.at[peer], ms.at[i], mr.at[i], other)
    came(idall.at[:, 1 - k], is_.at[4], ir.at[4], other)
    came(wfi.at[:, 1 - k], ws.at[8], wr.at[8], other)
    came(wfo.at[:, 1 - k], os_.at[8], or_.at[8], other)
    for (d, s), i in Z_INDEX.items():
        came(tabs.at[slot(d, s), :, 1 - k], cs.at[i], cr.at[i], other)
    for copy in sent:
        copy.wait_send()
    local[0].wait()
    local[4].wait()


def gather_all(tab, win, wout, ids, meta):
    return pl.pallas_call(
        gather_kernel,
        name="gather_all",
        out_shape=(
            jax.ShapeDtypeStruct((NZ, NY, 2, 128, COLS), BF),
            jax.ShapeDtypeStruct((NY, 2, NX, 16, 2048), BF),
            jax.ShapeDtypeStruct((NY, 2, NX, 16, 512), BF),
            jax.ShapeDtypeStruct((NY, 2, 8, TABLES, SLOT), jnp.int32),
            jax.ShapeDtypeStruct((NX, 8, 128), jnp.int32),
        ),
        in_specs=[VM] * 5,
        out_specs=(ANY,) * 5,
        scratch_shapes=[
            DMA((15,)), DMA((15,)), DMA((15, 4)), DMA((15, 4)), DMA((15,)), DMA((15,)),
            DMA((9,)), DMA((9,)), DMA((9,)), DMA((9,)), DMA((5,)), DMA((5,)),
            DMA((3,)), DMA((3,)), DMA((5,)),
        ],
        compiler_params=pltpu.CompilerParams(collective_id=0, has_side_effects=True),
    )(tab, win, wout, ids, meta)


def lookup_kernel(sel, *refs):
    slots, (table, out, columns, total) = refs[:8], refs[8:]
    t = pl.program_id(0)

    @pl.when(t == 0)
    def _():
        for i in range(8):
            columns[i * SLOT:(i + 1) * SLOT, :] = jnp.transpose(slots[i][0])
        total[...] = jnp.zeros_like(total)

    lane = lax.broadcasted_iota(jnp.int32, (8 * SLOT, TABLES), 1)
    picked = jnp.sum(jnp.where(lane == t, columns[...], 0), axis=1, keepdims=True)
    acc = total[...]
    for part in range(4):
        vocab = lax.broadcasted_iota(jnp.int32, (8 * SLOT, 256), 1) + part * 256
        hot = jnp.where(picked == vocab, 1.0, 0.0).astype(BF)
        acc = acc + jnp.dot(
            hot, table[0, part * 256:(part + 1) * 256, :], preferred_element_type=F32
        )
    total[...] = acc

    @pl.when(t == TABLES - 1)
    def _():
        out[...] = acc.astype(BF)


def slot_spec(i):
    return pl.BlockSpec((1, TABLES, SLOT), lambda t, sel: (sel[i], 0, 0))


def lookup(sel, ids, tables):
    return pl.pallas_call(
        lookup_kernel,
        name="lookup",
        out_shape=jax.ShapeDtypeStruct((8 * SLOT, COLS), BF),
        grid_spec=pltpu.PrefetchScalarGridSpec(
            num_scalar_prefetch=1,
            grid=(TABLES,),
            in_specs=[slot_spec(i) for i in range(8)]
            + [pl.BlockSpec((1, DISTINCT, COLS), lambda t, sel: (t, 0, 0))],
            out_specs=pl.BlockSpec((8 * SLOT, COLS), lambda t, sel: (0, 0)),
            scratch_shapes=[
                pltpu.VMEM((8 * SLOT, TABLES), jnp.int32),
                pltpu.VMEM((8 * SLOT, COLS), F32),
            ],
        ),
    )(sel, *([ids] * 8), tables)


def scatter_kernel(sel, *refs):
    slots, (grads, out, rows) = refs[:8], refs[8:]
    t = pl.program_id(0)

    @pl.when(t == 0)
    def _():
        for i in range(8):
            rows[:, i * SLOT:(i + 1) * SLOT] = slots[i][0]

    picked = rows[pl.ds(t, 1), :]
    for part in range(4):
        vocab = lax.broadcasted_iota(jnp.int32, (256, 8 * SLOT), 0) + part * 256
        hot = jnp.where(picked == vocab, 1.0, 0.0).astype(BF)
        out[0, part * 256:(part + 1) * 256, :] = jnp.dot(
            hot, grads[...], preferred_element_type=F32
        ).astype(BF)


def scatter(sel, ids, grads):
    return pl.pallas_call(
        scatter_kernel,
        name="scatter",
        out_shape=jax.ShapeDtypeStruct((TABLES, DISTINCT, COLS), BF),
        grid_spec=pltpu.PrefetchScalarGridSpec(
            num_scalar_prefetch=1,
            grid=(TABLES,),
            in_specs=[slot_spec(i) for i in range(8)]
            + [pl.BlockSpec((8 * SLOT, COLS), lambda t, sel: (0, 0))],
            out_specs=pl.BlockSpec((1, DISTINCT, COLS), lambda t, sel: (t, 0, 0)),
            scratch_shapes=[pltpu.VMEM((TABLES, 8 * SLOT), jnp.int32)],
        ),
    )(sel, *([ids] * 8), grads)


def exchange_kernel(forward, src, out, send, recv, loc):
    z, x, y, k = place()
    peers = [(x + 1) % NX, (x + 3) % NX, (x + 2) % NX]
    devices = [at(z, peer, y, k) for peer in peers]
    greet(devices)

    def piece(ref, i, split):
        if split:
            return ref.at[:, pl.ds(pl.multiple_of(i * COLS, COLS), COLS)]
        return ref.at[i]

    copies = []
    for i, (peer, device) in enumerate(zip(peers, devices)):
        copy = rcopy(
            piece(src, peer, not forward), piece(out, x, forward), send.at[i], recv.at[i], device
        )
        copy.start()
        copies.append(copy)
    own = pltpu.make_async_copy(piece(src, x, not forward), piece(out, x, forward), loc)
    own.start()
    for i, source in enumerate((peers[1], peers[0], peers[2])):
        landed = piece(out, source, forward)
        rcopy(landed, landed, send.at[i], recv.at[i], devices[i]).wait_recv()
    for copy in copies:
        copy.wait_send()
    own.wait()


def exchange(array, forward):
    shape = (256, D) if forward else (NX, 256, COLS)
    return pl.pallas_call(
        functools.partial(exchange_kernel, forward),
        name="exchange_rows" if forward else "exchange_grads",
        out_shape=jax.ShapeDtypeStruct(shape, BF),
        in_specs=[VM],
        out_specs=VM,
        scratch_shapes=[DMA((3,)), DMA((3,)), DMA],
        compiler_params=pltpu.CompilerParams(
            collective_id=1 if forward else 2, has_side_effects=True
        ),
    )(array)


def reduce_kernel(
    part, wg, tout, wout,
    t1, ta, tl1, tr1, tl2, tr2, tb, tz,
    w1, wa, wl1, wr1, wl2, wr2, wb, vl1, vr1, vl2, vr2, wc, wz, oz, wd, od, we,
    cs, cr, ys, yr, zs, zr, loc,
    wcs, wcr, wxs, wxr, wys, wyr, wzs, wzr, wgs, wgr, wes, wer,
):
    z, x, y, k = place()
    yp, ym, y2 = (y + 1) % NY, (y + 3) % NY, (y + 2) % NY
    xp, xm, x2 = (x + 1) % NX, (x + 3) % NX, (x + 2) % NX
    up, down = at(z, x, yp, k), at(z, x, ym, k)
    east, west, far = at(z, xp, y, k), at(z, xm, y, k), at(z, x2, y, k)
    other = at(z, x, y, 1 - k)
    ring = [(at((z + o) % NZ, x, y, k), (z + o) % NZ) for o in range(1, NZ)]
    greet([up, down, east, west, far, other] + [device for device, _ in ring])

    sent = []

    def go(src, dst, send, recv, device):
        copy = rcopy(src, dst, send, recv, device)
        copy.start()
        sent.append(copy)

    def came(dst, send, recv, device):
        rcopy(dst, dst, send, recv, device).wait_recv()

    def add(*values):
        total = values[0].astype(F32)
        for value in values[1:]:
            total = total + value.astype(F32)
        return total

    for c in range(4):
        go(part.at[:, c, :, 1 - k], t1.at[c], cs.at[c], cr.at[c], other)
        if c == 0:
            go(wg.at[:, 1 - k], w1, wcs, wcr, other)
    tload = pltpu.make_async_copy(part.at[:, :, :, k], ta, loc.at[0])
    tload.start()
    wload = pltpu.make_async_copy(wg.at[:, k], wa, loc.at[1])
    wload.start()

    def tables_core(c):
        came(t1.at[c], cs.at[c], cr.at[c], other)
        for i in range(4):
            ta[i, c] = add(ta[i, c], t1[c, i]).astype(BF)
        go(ta.at[:, c, y2, 0:64], tl1.at[c], ys.at[c, 0], yr.at[c, 0], up)
        go(ta.at[:, c, y2, 64:128], tr1.at[c], ys.at[c, 1], yr.at[c, 1], down)

    def tables_y(c):
        came(tl1.at[c], ys.at[c, 0], yr.at[c, 0], up)
        ta[:, c, yp, 0:64] = add(ta[:, c, yp, 0:64], tl1[c]).astype(BF)
        go(ta.at[:, c, yp], tl2.at[c], ys.at[c, 2], yr.at[c, 2], up)
        came(tr1.at[c], ys.at[c, 1], yr.at[c, 1], down)
        ta[:, c, ym, 64:128] = add(ta[:, c, ym, 64:128], tr1[c]).astype(BF)
        go(ta.at[:, c, ym], tr2.at[c], ys.at[c, 3], yr.at[c, 3], down)

    def tables_z(c):
        came(tl2.at[c], ys.at[c, 2], yr.at[c, 2], up)
        came(tr2.at[c], ys.at[c, 3], yr.at[c, 3], down)
        tb[c] = add(ta[:, c, y], tl2[c], tr2[c]).astype(BF)

    def tables_send(o):
        device, zz = ring[o - 1]
        go(tb.at[zz % 4, zz // 4], tz.at[o - 1], zs.at[o - 1], zr.at[o - 1], device)

    wload.wait()
    came(w1, wcs, wcr, other)
    for i in range(4):
        wa[i] = add(wa[i], w1[i]).astype(BF)
    go(wa.at[0:2, x2], wl1, wxs.at[0], wxr.at[0], east)
    go(wa.at[2:4, x2], wr1, wxs.at[1], wxr.at[1], west)
    tload.wait()
    tables_core(0)
    tables_core(1)
    came(wl1, wxs.at[0], wxr.at[0], east)
    wa[0:2, xp] = add(wa[0:2, xp], wl1[...]).astype(BF)
    go(wa.at[:, xp], wl2, wxs.at[2], wxr.at[2], east)
    came(wr1, wxs.at[1], wxr.at[1], west)
    wa[2:4, xm] = add(wa[2:4, xm], wr1[...]).astype(BF)
    go(wa.at[:, xm], wr2, wxs.at[3], wxr.at[3], west)
    tables_core(2)
    tables_core(3)
    tables_y(0)
    tables_y(1)
    came(wl2, wxs.at[2], wxr.at[2], east)
    came(wr2, wxs.at[3], wxr.at[3], west)
    wb[...] = add(wa[:, x], wl2[...], wr2[...]).astype(BF)
    go(wb.at[y2, :, 0:1280], vl1, wys.at[0], wyr.at[0], up)
    go(wb.at[y2, :, 1280:2560], vr1, wys.at[1], wyr.at[1], down)
    tables_y(2)
    tables_y(3)
    came(vl1, wys.at[0], wyr.at[0], up)
    wb[yp, :, 0:1280] = add(wb[yp, :, 0:1280], vl1[...]).astype(BF)
    go(wb.at[yp], vl2, wys.at[2], wyr.at[2], up)
    came(vr1, wys.at[1], wyr.at[1], down)
    wb[ym, :, 1280:2560] = add(wb[ym, :, 1280:2560], vr1[...]).astype(BF)
    go(wb.at[ym], vr2, wys.at[3], wyr.at[3], down)
    for c in range(4):
        tables_z(c)
    came(vl2, wys.at[2], wyr.at[2], up)
    came(vr2, wys.at[3], wyr.at[3], down)
    summed = add(wb[y], vl2[...], vr2[...]).astype(BF)
    for j in range(20):
        wc[j] = summed[:, j * 128:(j + 1) * 128]
    for o in (8, 7, 9, 6, 10, 5, 11, 4, 12, 3, 13, 2, 14, 1, 15):
        device, zz = ring[o - 1]
        go(wc.at[zz], wz.at[o - 1], wzs.at[o - 1, 0], wzr.at[o - 1, 0], device)
        go(wc.at[16 + zz // 4], oz.at[o - 1], wzs.at[o - 1, 1], wzr.at[o - 1, 1], device)
    for o in (8, 7, 9, 6, 10, 5, 11, 4, 12, 3, 13, 2, 14, 1, 15):
        tables_send(o)
    total_in = wc[z].astype(F32)
    total_out = wc[16 + z // 4].astype(F32)
    for o in range(1, NZ):
        came(wz.at[o - 1], wzs.at[o - 1, 0], wzr.at[o - 1, 0], other)
        came(oz.at[o - 1], wzs.at[o - 1, 1], wzr.at[o - 1, 1], other)
        total_in = total_in + wz[o - 1].astype(F32)
        total_out = total_out + oz[o - 1].astype(F32)
    wd[z] = total_in
    od[z] = total_out
    for o in (8, 7, 9, 6, 10, 5, 11, 4, 12, 3, 13, 2, 14, 1, 15):
        device, zz = ring[o - 1]
        go(wd.at[z], wd.at[z], wgs.at[o - 1, 0], wgr.at[o - 1, 0], device)
        go(od.at[z], od.at[z], wgs.at[o - 1, 1], wgr.at[o - 1, 1], device)
    for o in range(1, NZ):
        source = (z + NZ - o) % NZ
        came(wd.at[source], wgs.at[o - 1, 0], wgr.at[o - 1, 0], other)
        came(od.at[source], wgs.at[o - 1, 1], wgr.at[o - 1, 1], other)
    for j in range(16):
        we[:, j * 128:(j + 1) * 128] = wd[j]
    for c in range(4):
        we[:, 2048 + c * 128:2048 + (c + 1) * 128] = od[4 * c]
    for i, device in enumerate((east, west, far)):
        go(we, wout.at[x], wes.at[i], wer.at[i], device)
    own = pltpu.make_async_copy(we, wout.at[x], loc.at[2])
    own.start()
    total = tb[z % 4, z // 4].astype(F32)
    for o in range(1, NZ):
        came(tz.at[o - 1], zs.at[o - 1], zr.at[o - 1], other)
        total = total + tz[o - 1].astype(F32)
    tout[...] = total
    for i, source in enumerate((xm, xp, x2)):
        came(wout.at[source], wes.at[i], wer.at[i], other)
    own.wait()
    for copy in sent:
        copy.wait_send()


def reduce_all(part, wg):
    v = pltpu.VMEM
    return pl.pallas_call(
        reduce_kernel,
        name="reduce_all",
        out_shape=(
            jax.ShapeDtypeStruct((128, COLS), F32),
            jax.ShapeDtypeStruct((NX, 16, 2560), F32),
        ),
        in_specs=[ANY, ANY],
        out_specs=(VM, VM),
        scratch_shapes=[
            v((4, 4, NY, 128, COLS), BF), v((4, 4, NY, 128, COLS), BF),
            v((4, 4, 64, COLS), BF), v((4, 4, 64, COLS), BF),
            v((4, 4, 128, COLS), BF), v((4, 4, 128, COLS), BF),
            v((4, 4, 128, COLS), BF), v((15, 128, COLS), BF),
            v((NY, NX, 16, 2560), BF), v((NY, NX, 16, 2560), BF),
            v((2, 16, 2560), BF), v((2, 16, 2560), BF),
            v((4, 16, 2560), BF), v((4, 16, 2560), BF), v((4, 16, 2560), BF),
            v((16, 1280), BF), v((16, 1280), BF), v((16, 2560), BF), v((16, 2560), BF),
            v((20, 16, 128), BF), v((15, 16, 128), BF), v((15, 16, 128), BF),
            v((16, 16, 128), F32), v((16, 16, 128), F32), v((16, 2560), F32),
            DMA((4,)), DMA((4,)), DMA((4, 4)), DMA((4, 4)), DMA((15,)), DMA((15,)), DMA((3,)),
            DMA, DMA, DMA((4,)), DMA((4,)), DMA((4,)), DMA((4,)),
            DMA((15, 2)), DMA((15, 2)), DMA((15, 2)), DMA((15, 2)), DMA((3,)), DMA((3,)),
        ],
        compiler_params=pltpu.CompilerParams(
            collective_id=3, has_side_effects=True, vmem_limit_bytes=VMEM_LIMIT
        ),
    )(part, wg)


def silu_grad(argument):
    logistic = jax.nn.sigmoid(argument)
    return logistic * (1.0 + argument * (1.0 - logistic))


def normalize(values):
    average = jnp.mean(values, axis=1, keepdims=True)
    centred = values - average
    inverse = lax.rsqrt(jnp.mean(centred * centred, axis=1, keepdims=True) + EPS)
    return centred * inverse, inverse


def norm_back(incoming, normed, inverse):
    first = jnp.mean(incoming, axis=1, keepdims=True)
    second = jnp.mean(incoming * normed, axis=1, keepdims=True)
    return inverse * (incoming - first - normed * second)


def dot(a, b, ca, cb):
    return lax.dot_general(a, b, (((ca,), (cb,)), ((), ())), preferred_element_type=F32)


def layer_kernel(lengths, rows, cot, w_in, w_out, out, grad, pin, pout, act, proj, att, gh):
    width = D // HEADS
    scale = width ** (-0.5)
    values = rows[...].astype(F32)
    normed_in, in_inverse = normalize(values)
    half_in = normed_in.astype(BF)
    projected = dot(half_in, w_in[...], 1, 0)
    proj[...] = projected
    activated = jax.nn.silu(projected)
    gate = activated[:, :D]
    act[...] = activated[:, D:].astype(BF)
    place_i = lax.broadcasted_iota(jnp.int32, (SLOT, SLOT), 0)
    place_j = lax.broadcasted_iota(jnp.int32, (SLOT, SLOT), 1)
    masks = [(place_j <= place_i) & (place_i < lengths[s]) for s in range(NSEQ)]

    def heads(s, h):
        r = slice(s * SLOT, (s + 1) * SLOT)
        v = act[r, h * width:(h + 1) * width]
        q = act[r, D + h * width:D + (h + 1) * width]
        key = act[r, 2 * D + h * width:2 * D + (h + 1) * width]
        return r, v, q, key

    for s in range(NSEQ):
        for h in range(HEADS):
            r, v, q, key = heads(s, h)
            scores = dot(q, key, 1, 1) * scale
            weights = jnp.where(masks[s], jax.nn.silu(scores) * (1.0 / SLOT), 0.0).astype(BF)
            att[r, h * width:(h + 1) * width] = dot(weights, v, 1, 0)
    normed_out, out_inverse = normalize(att[...])
    mixed = (normed_out * gate).astype(BF)
    out[...] = (values + dot(mixed, w_out[...], 1, 0)).astype(BF)
    cotangent = cot[...]
    pout[...] = dot(mixed, cotangent, 0, 0).astype(BF)
    grad_mixed = dot(cotangent, w_out[...], 1, 1)
    att[...] = norm_back(grad_mixed * gate, normed_out, out_inverse)
    gh[:, :D] = (grad_mixed * normed_out * silu_grad(proj[:, :D])).astype(BF)
    for s in range(NSEQ):
        for h in range(HEADS):
            r, v, q, key = heads(s, h)
            g = att[r, h * width:(h + 1) * width].astype(BF)
            scores = dot(q, key, 1, 1) * scale
            logistic = jax.nn.sigmoid(scores)
            weights = jnp.where(masks[s], scores * logistic * (1.0 / SLOT), 0.0).astype(BF)
            slope = logistic * (1.0 + scores * (1.0 - logistic))
            gw = dot(g, v, 1, 1)
            gs = jnp.where(masks[s], gw * (1.0 / SLOT) * slope, 0.0).astype(BF)
            parts = (
                dot(weights, g, 0, 0), dot(gs, key, 1, 0) * scale, dot(gs, q, 0, 0) * scale
            )
            for p in range(3):
                c = slice(D + p * D + h * width, D + p * D + (h + 1) * width)
                gh[r, c] = (parts[p] * silu_grad(proj[r, c])).astype(BF)
    grad_projected = gh[...]
    pin[...] = dot(half_in, grad_projected, 0, 0).astype(BF)
    grad_normed = dot(grad_projected, w_in[...], 1, 1)
    grad[...] = (
        cotangent.astype(F32) + norm_back(grad_normed, normed_in, in_inverse)
    ).astype(BF)


def layer(lengths, rows, cot, w_in, w_out):
    v = pltpu.VMEM
    return pl.pallas_call(
        layer_kernel,
        name="layer",
        out_shape=(
            jax.ShapeDtypeStruct((256, D), BF),
            jax.ShapeDtypeStruct((256, D), BF),
            jax.ShapeDtypeStruct((D, 4 * D), BF),
            jax.ShapeDtypeStruct((D, D), BF),
        ),
        in_specs=[pl.BlockSpec(memory_space=pltpu.SMEM)] + [VM] * 4,
        out_specs=(VM,) * 4,
        scratch_shapes=[
            v((256, 3 * D), BF), v((256, 4 * D), F32), v((256, D), F32), v((256, 4 * D), BF),
        ],
        compiler_params=pltpu.CompilerParams(vmem_limit_bytes=VMEM_LIMIT),
    )(lengths, rows, cot, w_in, w_out)


def on_device(
    item_ids, seq_lengths, surplus_slot, helper_map, embed_tables, weight_in, weight_out, cotangent
):
    z, x, y, k = place()
    bal = lax.axis_index("bal")
    near = lax.dynamic_slice_in_dim(item_ids[0], z * 1024, 1024, 0)
    ids = jnp.transpose(near.reshape(8, SLOT, TABLES), (0, 2, 1))
    meta = jnp.concatenate(
        [seq_lengths.reshape(16), surplus_slot.reshape(8), helper_map.reshape(8)]
    )
    meta = jnp.broadcast_to(jnp.pad(meta, (0, 96))[None], (8, 128))
    tabs, w_in, w_out, id_all, meta_all = gather_all(
        embed_tables.reshape(NY, 2, 128, COLS),
        weight_in.reshape(NX, 16, 2048),
        weight_out.reshape(NX, 16, 512),
        ids,
        meta,
    )
    facts = meta_all[:, 0, :32]
    lengths = facts[:, :16].reshape(NX, NB, NSEQ)
    surplus = facts[:, 16:24]
    helper = facts[:, 24:32]
    bals = jnp.arange(NB, dtype=jnp.int32)[None]
    is_source = helper == bal
    source = jnp.sum(jnp.where(is_source, bals, 0), axis=1)
    source_slot = jnp.sum(jnp.where(is_source, surplus, 0), axis=1)
    my_slot = jnp.sum(jnp.where(bals == bal, surplus, 0), axis=1)
    slots = jnp.arange(NSEQ, dtype=jnp.int32)[None]
    xs = jnp.arange(NX, dtype=jnp.int32)
    moved = slots == my_slot[:, None]
    sel = jnp.where(
        moved, (source * 8 + xs * 2 + source_slot)[:, None], bal * 8 + xs[:, None] * 2 + slots
    ).reshape(8)
    own_lengths = jnp.sum(jnp.where((bals == bal)[:, :, None], lengths, 0), axis=1)
    moved_length = jnp.sum(
        jnp.where(
            is_source[:, :, None] & (slots[None] == source_slot[:, None, None]), lengths, 0
        ),
        axis=(1, 2),
    )
    proc_lengths = jnp.where(moved, moved_length[:, None], own_lengths)
    my_lengths = jnp.sum(jnp.where(xs[:, None] == x, proc_lengths, 0), axis=0)

    id_flat = id_all.reshape(64, TABLES, SLOT)
    looked = lookup(sel, id_flat, tabs.reshape(TABLES, DISTINCT, COLS))
    rows = exchange(looked.reshape(NX, 256, COLS), True)
    forward_out, grad_rows, partial_in, partial_out = layer(
        my_lengths, rows, cotangent[0], w_in.reshape(D, 4 * D), w_out.reshape(D, D)
    )
    columns = exchange(grad_rows, False)
    part = scatter(sel, id_flat, columns.reshape(1024, COLS))
    wg = jnp.concatenate([partial_in, partial_out], axis=1).reshape(NY, 2, NX, 16, 2560)
    table_sum, weight_sum = reduce_all(part.reshape(4, 4, NY, 2, 128, COLS), wg)
    events = NB * item_ids.shape[1]
    table_scale = (DISTINCT / events) ** 0.5
    grad_scale = events ** (-0.5)
    weight_sum = weight_sum.reshape(64, 2560)
    return (
        forward_out[None],
        (table_sum * table_scale)[None],
        weight_sum[:, :2048] * grad_scale,
        weight_sum[:, 2048:] * grad_scale,
    )


def solution(mesh):
    placed = (
        P("bal", None, None),
        P(None, "emb", None),
        P(None, "emb"),
        P(None, "emb"),
        P("emb", None, None),
        P("bal", None),
        P("bal", None),
        P("bal", "emb", None),
    )
    return jax.shard_map(
        on_device,
        mesh=mesh,
        in_specs=placed,
        out_specs=(P("bal", "emb", None), P("emb", "bal", None), P("bal", None), P("bal", None)),
        check_vma=False,
    )
```

time: 1070 us -> 221 us (0.21)
  waiting for transfers between devices: 381 us -> 0 us
  blocking collectives: 373 us -> 0 us
  Pallas kernels: 0 us -> 202 us
  other arithmetic: 112 us -> 10.4 us
  local copies, waits for them, and re-layouts: 96.7 us -> 3.77 us
  matrix products: 35.4 us -> 0 us
  starting transfers between devices: 35.2 us -> 0 us
  between operations: 20 us -> 0.74 us
  loops' own time: 11.1 us -> 0 us
    psum x1 -> x0, blocking collectives: 359 us -> none  [on_device(): total_in, total_out = lax.psum((owned_in, owned_out), 'emb')]
    pallas_call x0 -> x7, Pallas kernels: none -> 202 us  [the longest x1 88.7 us: reduce_all(): pl.pallas_call(reduce_kernel, name='reduce_all', out_shape=(jax.ShapeDtyp...]
    all_to_all x2 -> x0, waiting for transfers between devices: 185 us -> none  [the longest x1 185 us: on_device(): lax.all_to_all(looked, 'emb', split_axis=0, concat_axis=1, tiled=True)]
    reduce_scatter x3 -> x0, waiting for transfers between devices: 127 us -> none  [the longest x1 44.5 us: on_device(): lax.psum_scatter(table_part.astype(jnp.bfloat16), 'bal', scatter_dimensio...]
    scatter-add x1 -> x0, other arithmetic: 87.7 us -> none  [on_device(): jnp.zeros((DISTINCT, COLS), jnp.float32).at[table_ids]]
    all_gather x3 -> x0, waiting for transfers between devices: 67.9 us -> none  [the longest x1 33.8 us: on_device(): lax.all_gather(weight_in, 'bal', axis=0, tiled=True)]
    gather x1 -> x0, local copies, waits for them, and re-layouts: 57.4 us -> none  [on_device(): looked = embed_tables[0][table_ids]]
    dot_general x54 -> x0, matrix products: 35.4 us -> none  [the longest x8 7.38 us: head_backward(): jnp.dot(silu_weights.T, grad_head, preferred_element_type=jnp.float32)]
  transfers between devices with their start and end apart: 8 -> 0, of which waited for: 7 -> 0; matrix products, arithmetic and copies ran while one was open for 1% -> 0% of each run, Pallas kernels for 0% -> 0%
where the time goes in v1:
time: 221 us; the launch traced here: 217 us
  Pallas kernels  202 us (91%)
  other arithmetic  10.4 us (5%)
  local copies, waits for them, and re-layouts  3.77 us (2%)
    pallas_call x1, Pallas kernels, reduce_all(): pl.pallas_call(reduce_kernel, name='reduce_all', out_shape=(jax.ShapeDtyp...  88.7 us
    pallas_call x1, Pallas kernels, gather_all(): pl.pallas_call(gather_kernel, name='gather_all', out_shape=(jax.ShapeDtyp...  49.9 us
    pallas_call x2, Pallas kernels, exchange(): pl.pallas_call(functools.partial(exchange_kernel, forward), name='exchang...  19 us
    pallas_call x1, Pallas kernels, lookup(): pl.pallas_call(lookup_kernel, name='lookup', out_shape=jax.ShapeDtypeStru...  17.4 us
    pallas_call x1, Pallas kernels, scatter(): pl.pallas_call(scatter_kernel, name='scatter', out_shape=jax.ShapeDtypeSt...  14.6 us
    pallas_call x1, Pallas kernels, layer(): pl.pallas_call(layer_kernel, name='layer', out_shape=(jax.ShapeDtypeStruc...  12.7 us

profile of v1, /device:TPU:6, one launch (start us, length us, event | category | flops | bytes accessed | tf_op | source)
XLA Modules:
  0.0 217.3 jit_solution(11277173471976877134)
XLA Ops:
  0.6 0.0 copy-start
  0.7 0.8 copy.18
  1.5 0.1 reshape.132
  1.6 0.7 pad_add_fusion
  2.4 0.6 broadcast_in_dim.89.meta
  3.0 0.0 copy-done
  3.0 0.6 copy.23
  3.6 49.9 %gather_all.1 = (bf16[16,4,2,128,128]{4,3,2,1,0:T(8,128)(2,1)}, bf16[4,2,4,16,2048]{4,3,2,1,0:T(8,128)(2,1)}, bf16[4,2,4,16,512]{4,3,2,1,0:T(8,128)(2,1)}, s32[4,2,8,16,128]{4,3,2,1,0:T(8,128)}, s32[4,8,128]{2,1,0:T(8,128)}) custom-call(bf16[4,2,128,128]{3,2,1,0:T(8,128)(2,1)} %bitcast.57, bf16[4,16,2048]{2,1,0:T(8,128)(2,1)} %bitcast.58, ...), custom_call_target="tpu_custom_call" | custom-call | tf_op jit(solution)/shard_map/gather_all/pallas_call | solution.py:204
  53.6 0.7 slice.18
  54.3 0.2 select_reduce_fusion.4
  54.5 0.1 iota_compare_fusion
  54.6 0.1 broadcast_and_fusion
  54.7 0.1 and.34
  54.8 0.1 select_reduce_fusion.2
  54.9 0.1 copy.19
  55.0 0.1 select_reduce_fusion
  55.1 0.6 add_select_fusion
  55.7 0.1 copy.20
  55.8 0.6 select_n.61.sel
  56.4 17.4 %lookup.1 = bf16[1024,128]{1,0:T(8,128)(2,1)} custom-call(s32[8]{0:T(128)} %select_n.61.sel, s32[64,16,128]{2,1,0:T(8,128)} %bitcast.31, s32[64,16,128]{2,1,0:T(8,128)} %bitcast.32, s32[64,16,128]{2,1,0:T(8,128)} %bitcast.33, s32[64,16,128]{2,1,0:T(8,128)} %bitcast.34, s32[64,16,128]{2,1,0:T(8,128)} %bitcast.35, s32[64,16,128]{2,1,0:T(8,128)} %bitcast.36, ...), custom_call_target="tpu_custom_call" | custom-call | tf_op jit(solution)/shard_map/lookup/pallas_call | solution.py:256
  73.8 10.0 %exchange_rows.1.rows = bf16[256,512]{1,0:T(8,128)(2,1)} custom-call(bf16[4,256,128]{2,1,0:T(8,128)(2,1)} %bitcast.52), custom_call_target="tpu_custom_call" | custom-call | tf_op jit(solution)/shard_map/exchange_rows/pallas_call | solution.py:338
  83.8 12.7 %layer.1 = (bf16[256,512]{1,0:T(8,128)(2,1)}, bf16[256,512]{1,0:T(8,128)(2,1)}, bf16[512,2048]{1,0:T(8,128)(2,1)}, bf16[512,512]{1,0:T(8,128)(2,1)}) custom-call(s32[2]{0:T(128)} %get-tuple-element.33.lengths, bf16[256,512]{1,0:T(8,128)(2,1)} %exchange_rows.1.rows, bf16[256,512]{1,0:T(8,128)(2,1)} %bitcast.60, bf16[512,2048]{1,0:T(8,128)(2,1)} %bitcast.50, ...), custom_call_target="tpu_custom_call" | custom-call | tf_op jit(solution)/shard_map/layer/pallas_call | solution.py:614
  96.5 9.0 %exchange_grads.1 = bf16[4,256,128]{2,1,0:T(8,128)(2,1)} custom-call(bf16[256,512]{1,0:T(8,128)(2,1)} %get-tuple-element.21.src), custom_call_target="tpu_custom_call" | custom-call | tf_op jit(solution)/shard_map/exchange_grads/pallas_call | solution.py:338
  105.6 3.5 %pad_maximum_fusion = bf16[512,2560]{1,0:T(8,128)(2,1)} fusion(bf16[512,512]{1,0:T(8,128)(2,1)} %get-tuple-element.23, bf16[512,2048]{1,0:T(8,128)(2,1)} %get-tuple-element.22), kind=kLoop, calls=%fused_computation | loop fusion | flops 5242880 | bytes 5242880 | tf_op jit(solution)/shard_map/concatenate | solution.py:683
  109.0 14.6 %scatter.1 = bf16[16,1024,128]{2,1,0:T(8,128)(2,1)} custom-call(s32[8]{0:T(128)} %select_n.61.sel, s32[64,16,128]{2,1,0:T(8,128)} %bitcast.39, s32[64,16,128]{2,1,0:T(8,128)} %bitcast.40, s32[64,16,128]{2,1,0:T(8,128)} %bitcast.41, s32[64,16,128]{2,1,0:T(8,128)} %bitcast.42, s32[64,16,128]{2,1,0:T(8,128)} %bitcast.43, s32[64,16,128]{2,1,0:T(8,128)} %bitcast.44, ...), custom_call_target="tpu_custom_call" | custom-call | tf_op jit(solution)/shard_map/scatter/pallas_call | solution.py:293
  123.6 88.7 %reduce_all.1 = (f32[128,128]{1,0:T(8,128)}, f32[4,16,2560]{2,1,0:T(8,128)}) custom-call(bf16[4,4,4,2,128,128]{5,4,3,2,1,0:T(8,128)(2,1)} %bitcast.47, bf16[4,2,4,16,2560]{4,3,2,1,0:T(8,128)(2,1)} %bitcast.48), custom_call_target="tpu_custom_call" | custom-call | tf_op jit(solution)/shard_map/reduce_all/pallas_call | solution.py:500
  212.3 1.5 multiply_bitcast_fusion
  213.8 1.6 slice_multiply_fusion.1
  215.4 1.9 slice_multiply_fusion
  (6 shorter events, 0.0 us)
Async XLA Ops:
  0.6 2.3 %copy-start = (s32[1,16384,16]{1,2,0:T(8,128)S(1)}, s32[1,16384,16]{1,2,0:T(8,128)}, u32[]{:S(2)}) copy-start(s32[1,16384,16]{1,2,0:T(8,128)} %param.8) | copy-start | bytes 3145732

commit v2 on v1

--- a/solution.py
+++ b/solution.py
@@ -223,12 +223,13 @@
 
 
 def lookup_kernel(sel, *refs):
-    slots, (table, out, columns, total) = refs[:8], refs[8:]
+    slots, (table, out, rows, columns, total) = refs[:8], refs[8:]
     t = pl.program_id(0)
 
     @pl.when(t == 0)
     def _():
         for i in range(8):
+            rows[:, i * SLOT:(i + 1) * SLOT] = slots[i][0]
             columns[i * SLOT:(i + 1) * SLOT, :] = jnp.transpose(slots[i][0])
         total[...] = jnp.zeros_like(total)
 
@@ -256,13 +257,19 @@
     return pl.pallas_call(
         lookup_kernel,
         name="lookup",
-        out_shape=jax.ShapeDtypeStruct((8 * SLOT, COLS), BF),
+        out_shape=(
+            jax.ShapeDtypeStruct((8 * SLOT, COLS), BF),
+            jax.ShapeDtypeStruct((TABLES, 8 * SLOT), jnp.int32),
+        ),
         grid_spec=pltpu.PrefetchScalarGridSpec(
             num_scalar_prefetch=1,
             grid=(TABLES,),
             in_specs=[slot_spec(i) for i in range(8)]
             + [pl.BlockSpec((1, DISTINCT, COLS), lambda t, sel: (t, 0, 0))],
-            out_specs=pl.BlockSpec((8 * SLOT, COLS), lambda t, sel: (0, 0)),
+            out_specs=(
+                pl.BlockSpec((8 * SLOT, COLS), lambda t, sel: (0, 0)),
+                pl.BlockSpec((TABLES, 8 * SLOT), lambda t, sel: (0, 0)),
+            ),
             scratch_shapes=[
                 pltpu.VMEM((8 * SLOT, TABLES), jnp.int32),
                 pltpu.VMEM((8 * SLOT, COLS), F32),
@@ -271,88 +278,52 @@
     )(sel, *([ids] * 8), tables)
 
 
-def scatter_kernel(sel, *refs):
-    slots, (grads, out, rows) = refs[:8], refs[8:]
-    t = pl.program_id(0)
-
-    @pl.when(t == 0)
-    def _():
-        for i in range(8):
-            rows[:, i * SLOT:(i + 1) * SLOT] = slots[i][0]
-
-    picked = rows[pl.ds(t, 1), :]
-    for part in range(4):
-        vocab = lax.broadcasted_iota(jnp.int32, (256, 8 * SLOT), 0) + part * 256
-        hot = jnp.where(picked == vocab, 1.0, 0.0).astype(BF)
-        out[0, part * 256:(part + 1) * 256, :] = jnp.dot(
-            hot, grads[...], preferred_element_type=F32
-        ).astype(BF)
-
-
-def scatter(sel, ids, grads):
-    return pl.pallas_call(
-        scatter_kernel,
-        name="scatter",
-        out_shape=jax.ShapeDtypeStruct((TABLES, DISTINCT, COLS), BF),
-        grid_spec=pltpu.PrefetchScalarGridSpec(
-            num_scalar_prefetch=1,
-            grid=(TABLES,),
-            in_specs=[slot_spec(i) for i in range(8)]
-            + [pl.BlockSpec((8 * SLOT, COLS), lambda t, sel: (0, 0))],
-            out_specs=pl.BlockSpec((1, DISTINCT, COLS), lambda t, sel: (t, 0, 0)),
-            scratch_shapes=[pltpu.VMEM((TABLES, 8 * SLOT), jnp.int32)],
-        ),
-    )(sel, *([ids] * 8), grads)
-
-
-def exchange_kernel(forward, src, out, send, recv, loc):
+def exchange_kernel(src, out, send, recv, loc):
     z, x, y, k = place()
     peers = [(x + 1) % NX, (x + 3) % NX, (x + 2) % NX]
     devices = [at(z, peer, y, k) for peer in peers]
     greet(devices)
 
-    def piece(ref, i, split):
-        if split:
-            return ref.at[:, pl.ds(pl.multiple_of(i * COLS, COLS), COLS)]
-        return ref.at[i]
+    def piece(i):
+        return out.at[:, pl.ds(pl.multiple_of(i * COLS, COLS), COLS)]
 
     copies = []
     for i, (peer, device) in enumerate(zip(peers, devices)):
-        copy = rcopy(
-            piece(src, peer, not forward), piece(out, x, forward), send.at[i], recv.at[i], device
-        )
+        copy = rcopy(src.at[peer], piece(x), send.at[i], recv.at[i], device)
         copy.start()
         copies.append(copy)
-    own = pltpu.make_async_copy(piece(src, x, not forward), piece(out, x, forward), loc)
+    own = pltpu.make_async_copy(src.at[x], piece(x), loc)
     own.start()
     for i, source in enumerate((peers[1], peers[0], peers[2])):
-        landed = piece(out, source, forward)
+        landed = piece(source)
         rcopy(landed, landed, send.at[i], recv.at[i], devices[i]).wait_recv()
     for copy in copies:
         copy.wait_send()
     own.wait()
 
 
-def exchange(array, forward):
-    shape = (256, D) if forward else (NX, 256, COLS)
+def exchange(array):
     return pl.pallas_call(
-        functools.partial(exchange_kernel, forward),
-        name="exchange_rows" if forward else "exchange_grads",
-        out_shape=jax.ShapeDtypeStruct(shape, BF),
+        exchange_kernel,
+        name="exchange_rows",
+        out_shape=jax.ShapeDtypeStruct((256, D), BF),
         in_specs=[VM],
         out_specs=VM,
         scratch_shapes=[DMA((3,)), DMA((3,)), DMA],
-        compiler_params=pltpu.CompilerParams(
-            collective_id=1 if forward else 2, has_side_effects=True
-        ),
+        compiler_params=pltpu.CompilerParams(collective_id=1, has_side_effects=True),
     )(array)
 
 
-def reduce_kernel(
-    part, wg, tout, wout,
-    t1, ta, tl1, tr1, tl2, tr2, tb, tz,
-    w1, wa, wl1, wr1, wl2, wr2, wb, vl1, vr1, vl2, vr2, wc, wz, oz, wd, od, we,
-    cs, cr, ys, yr, zs, zr, loc,
+OFFSETS = (2, 1, -1, 0)
+FAR_FIRST = (8, 7, 9, 6, 10, 5, 11, 4, 12, 3, 13, 2, 14, 1, 15)
+
+
+def back_kernel(
+    table_scale, grad_scale,
+    grads, rows, wg, tout, win_out, wout_out,
+    gx, to, t1, ta, tl1, tr1, tl2, tr2, tb, tz1, ts, tz2,
+    w1, wa, wl1, wr1, wl2, wr2, wb, vl1, vr1, vl2, vr2, wc, wz, wd, we,
+    gs, gr, cs, cr, ys, yr, zs, zr, z2s, z2r, loc,
     wcs, wcr, wxs, wxr, wys, wyr, wzs, wzr, wgs, wgr, wes, wer,
 ):
     z, x, y, k = place()
@@ -361,8 +332,8 @@
     up, down = at(z, x, yp, k), at(z, x, ym, k)
     east, west, far = at(z, xp, y, k), at(z, xm, y, k), at(z, x2, y, k)
     other = at(z, x, y, 1 - k)
-    ring = [(at((z + o) % NZ, x, y, k), (z + o) % NZ) for o in range(1, NZ)]
-    greet([up, down, east, west, far, other] + [device for device, _ in ring])
+    ring = {o: (z + o) % NZ for o in range(1, NZ)}
+    greet([up, down, east, west, far, other] + [at(ring[o], x, y, k) for o in range(1, NZ)])
 
     sent = []
 
@@ -371,8 +342,8 @@
         copy.start()
         sent.append(copy)
 
-    def came(dst, send, recv, device):
-        rcopy(dst, dst, send, recv, device).wait_recv()
+    def came(dst, send, recv):
+        rcopy(dst, dst, send, recv, other).wait_recv()
 
     def add(*values):
         total = values[0].astype(F32)
@@ -380,151 +351,229 @@
             total = total + value.astype(F32)
         return total
 
-    for c in range(4):
-        go(part.at[:, c, :, 1 - k], t1.at[c], cs.at[c], cr.at[c], other)
-        if c == 0:
-            go(wg.at[:, 1 - k], w1, wcs, wcr, other)
-    tload = pltpu.make_async_copy(part.at[:, :, :, k], ta, loc.at[0])
-    tload.start()
+    def columns(i):
+        return grads.at[:, pl.ds(pl.multiple_of(i * COLS, COLS), COLS)]
+
+    for i, (peer, device) in enumerate(((x2, far), (xp, east), (xm, west))):
+        go(columns(peer), gx.at[x], gs.at[i], gr.at[i], device)
+    own = pltpu.make_async_copy(columns(x), gx.at[x], loc.at[0])
+    own.start()
+    go(wg.at[:, 1 - k], w1, wcs, wcr, other)
     wload = pltpu.make_async_copy(wg.at[:, k], wa, loc.at[1])
     wload.start()
 
-    def tables_core(c):
-        came(t1.at[c], cs.at[c], cr.at[c], other)
+    place_row = lax.broadcasted_iota(jnp.int32, (128, 8 * SLOT), 0)
+
+    def rows_of(q, core, out):
+        residue = (z + OFFSETS[q] + NZ) % 4
+
+        def body(i, carry):
+            picked = rows[pl.ds(i * 4 + residue, 1), :] - core * 128
+            hot = jnp.concatenate(
+                [
+                    jnp.where(picked - part * 256 == place_row, 1.0, 0.0).astype(BF)
+                    for part in range(4)
+                ],
+                axis=0,
+            )
+            found = jnp.dot(
+                hot, gx[...].reshape(8 * SLOT, COLS), preferred_element_type=F32
+            ).astype(BF)
+            out[q, i] = found.reshape(NY, 128, COLS)
+            return carry
+
+        lax.fori_loop(0, 4, body, 0)
+
+    def compute(q):
+        rows_of(q, 1 - k, to)
+        go(to.at[q], t1.at[q], cs.at[q], cr.at[q], other)
+        rows_of(q, k, ta)
+
+    def t_core(q):
+        came(t1.at[q], cs.at[q], cr.at[q])
         for i in range(4):
-            ta[i, c] = add(ta[i, c], t1[c, i]).astype(BF)
-        go(ta.at[:, c, y2, 0:64], tl1.at[c], ys.at[c, 0], yr.at[c, 0], up)
-        go(ta.at[:, c, y2, 64:128], tr1.at[c], ys.at[c, 1], yr.at[c, 1], down)
-
-    def tables_y(c):
-        came(tl1.at[c], ys.at[c, 0], yr.at[c, 0], up)
-        ta[:, c, yp, 0:64] = add(ta[:, c, yp, 0:64], tl1[c]).astype(BF)
-        go(ta.at[:, c, yp], tl2.at[c], ys.at[c, 2], yr.at[c, 2], up)
-        came(tr1.at[c], ys.at[c, 1], yr.at[c, 1], down)
-        ta[:, c, ym, 64:128] = add(ta[:, c, ym, 64:128], tr1[c]).astype(BF)
-        go(ta.at[:, c, ym], tr2.at[c], ys.at[c, 3], yr.at[c, 3], down)
-
-    def tables_z(c):
-        came(tl2.at[c], ys.at[c, 2], yr.at[c, 2], up)
-        came(tr2.at[c], ys.at[c, 3], yr.at[c, 3], down)
-        tb[c] = add(ta[:, c, y], tl2[c], tr2[c]).astype(BF)
-
-    def tables_send(o):
-        device, zz = ring[o - 1]
-        go(tb.at[zz % 4, zz // 4], tz.at[o - 1], zs.at[o - 1], zr.at[o - 1], device)
-
-    wload.wait()
-    came(w1, wcs, wcr, other)
-    for i in range(4):
-        wa[i] = add(wa[i], w1[i]).astype(BF)
-    go(wa.at[0:2, x2], wl1, wxs.at[0], wxr.at[0], east)
-    go(wa.at[2:4, x2], wr1, wxs.at[1], wxr.at[1], west)
-    tload.wait()
-    tables_core(0)
-    tables_core(1)
-    came(wl1, wxs.at[0], wxr.at[0], east)
-    wa[0:2, xp] = add(wa[0:2, xp], wl1[...]).astype(BF)
-    go(wa.at[:, xp], wl2, wxs.at[2], wxr.at[2], east)
-    came(wr1, wxs.at[1], wxr.at[1], west)
-    wa[2:4, xm] = add(wa[2:4, xm], wr1[...]).astype(BF)
-    go(wa.at[:, xm], wr2, wxs.at[3], wxr.at[3], west)
-    tables_core(2)
-    tables_core(3)
-    tables_y(0)
-    tables_y(1)
-    came(wl2, wxs.at[2], wxr.at[2], east)
-    came(wr2, wxs.at[3], wxr.at[3], west)
-    wb[...] = add(wa[:, x], wl2[...], wr2[...]).astype(BF)
-    go(wb.at[y2, :, 0:1280], vl1, wys.at[0], wyr.at[0], up)
-    go(wb.at[y2, :, 1280:2560], vr1, wys.at[1], wyr.at[1], down)
-    tables_y(2)
-    tables_y(3)
-    came(vl1, wys.at[0], wyr.at[0], up)
-    wb[yp, :, 0:1280] = add(wb[yp, :, 0:1280], vl1[...]).astype(BF)
-    go(wb.at[yp], vl2, wys.at[2], wyr.at[2], up)
-    came(vr1, wys.at[1], wyr.at[1], down)
-    wb[ym, :, 1280:2560] = add(wb[ym, :, 1280:2560], vr1[...]).astype(BF)
-    go(wb.at[ym], vr2, wys.at[3], wyr.at[3], down)
-    for c in range(4):
-        tables_z(c)
-    came(vl2, wys.at[2], wyr.at[2], up)
-    came(vr2, wys.at[3], wyr.at[3], down)
-    summed = add(wb[y], vl2[...], vr2[...]).astype(BF)
-    for j in range(20):
-        wc[j] = summed[:, j * 128:(j + 1) * 128]
-    for o in (8, 7, 9, 6, 10, 5, 11, 4, 12, 3, 13, 2, 14, 1, 15):
-        device, zz = ring[o - 1]
-        go(wc.at[zz], wz.at[o - 1], wzs.at[o - 1, 0], wzr.at[o - 1, 0], device)
-        go(wc.at[16 + zz // 4], oz.at[o - 1], wzs.at[o - 1, 1], wzr.at[o - 1, 1], device)
-    for o in (8, 7, 9, 6, 10, 5, 11, 4, 12, 3, 13, 2, 14, 1, 15):
-        tables_send(o)
-    total_in = wc[z].astype(F32)
-    total_out = wc[16 + z // 4].astype(F32)
-    for o in range(1, NZ):
-        came(wz.at[o - 1], wzs.at[o - 1, 0], wzr.at[o - 1, 0], other)
-        came(oz.at[o - 1], wzs.at[o - 1, 1], wzr.at[o - 1, 1], other)
-        total_in = total_in + wz[o - 1].astype(F32)
-        total_out = total_out + oz[o - 1].astype(F32)
-    wd[z] = total_in
-    od[z] = total_out
-    for o in (8, 7, 9, 6, 10, 5, 11, 4, 12, 3, 13, 2, 14, 1, 15):
-        device, zz = ring[o - 1]
-        go(wd.at[z], wd.at[z], wgs.at[o - 1, 0], wgr.at[o - 1, 0], device)
-        go(od.at[z], od.at[z], wgs.at[o - 1, 1], wgr.at[o - 1, 1], device)
-    for o in range(1, NZ):
-        source = (z + NZ - o) % NZ
-        came(wd.at[source], wgs.at[o - 1, 0], wgr.at[o - 1, 0], other)
-        came(od.at[source], wgs.at[o - 1, 1], wgr.at[o - 1, 1], other)
-    for j in range(16):
-        we[:, j * 128:(j + 1) * 128] = wd[j]
-    for c in range(4):
-        we[:, 2048 + c * 128:2048 + (c + 1) * 128] = od[4 * c]
-    for i, device in enumerate((east, west, far)):
-        go(we, wout.at[x], wes.at[i], wer.at[i], device)
-    own = pltpu.make_async_copy(we, wout.at[x], loc.at[2])
-    own.start()
-    total = tb[z % 4, z // 4].astype(F32)
-    for o in range(1, NZ):
-        came(tz.at[o - 1], zs.at[o - 1], zr.at[o - 1], other)
-        total = total + tz[o - 1].astype(F32)
-    tout[...] = total
-    for i, source in enumerate((xm, xp, x2)):
-        came(wout.at[source], wes.at[i], wer.at[i], other)
+            ta[q, i] = add(ta[q, i], t1[q, i]).astype(BF)
+        go(ta.at[q, :, y2, 0:64], tl1.at[q], ys.at[q, 0], yr.at[q, 0], up)
+        go(ta.at[q, :, y2, 64:128], tr1.at[q], ys.at[q, 1], yr.at[q, 1], down)
+
+    def t_y(q):
+        came(tl1.at[q], ys.at[q, 0], yr.at[q, 0])
+        ta[q, :, yp, 0:64] = add(ta[q, :, yp, 0:64], tl1[q]).astype(BF)
+        go(ta.at[q, :, yp], tl2.at[q], ys.at[q, 2], yr.at[q, 2], up)
+        came(tr1.at[q], ys.at[q, 1], yr.at[q, 1])
+        ta[q, :, ym, 64:128] = add(ta[q, :, ym, 64:128], tr1[q]).astype(BF)
+        go(ta.at[q, :, ym], tr2.at[q], ys.at[q, 3], yr.at[q, 3], down)
+
+    def t_z(q):
+        came(tl2.at[q], ys.at[q, 2], yr.at[q, 2])
+        came(tr2.at[q], ys.at[q, 3], yr.at[q, 3])
+        tb[q] = add(ta[q, :, y], tl2[q], tr2[q]).astype(BF)
+        if q < 3:
+            device = at((z + OFFSETS[q] + NZ) % NZ, x, y, k)
+            go(tb.at[q], tz1.at[q], zs.at[q], zr.at[q], device)
+
+    def t_z2():
+        for q in range(3):
+            came(tz1.at[q], zs.at[q], zr.at[q])
+        ts[...] = add(tb[3], tz1[0], tz1[1], tz1[2]).astype(BF)
+        for m in (2, 1, 3):
+            zz = (z + 4 * m) % NZ
+            go(ts.at[zz // 4], tz2.at[m - 1], z2s.at[m - 1], z2r.at[m - 1], at(zz, x, y, k))
+
+    def t_end():
+        total = ts[z // 4].astype(F32)
+        for m in range(3):
+            came(tz2.at[m], z2s.at[m], z2r.at[m])
+            total = total + tz2[m].astype(F32)
+        tout[...] = total * table_scale
+
+    def w_core():
+        wload.wait()
+        came(w1, wcs, wcr)
+        for i in range(4):
+            wa[i] = add(wa[i], w1[i]).astype(BF)
+        go(wa.at[0:2, x2], wl1, wxs.at[0], wxr.at[0], east)
+        go(wa.at[2:4, x2], wr1, wxs.at[1], wxr.at[1], west)
+
+    def w_x():
+        came(wl1, wxs.at[0], wxr.at[0])
+        wa[0:2, xp] = add(wa[0:2, xp], wl1[...]).astype(BF)
+        go(wa.at[:, xp], wl2, wxs.at[2], wxr.at[2], east)
+        came(wr1, wxs.at[1], wxr.at[1])
+        wa[2:4, xm] = add(wa[2:4, xm], wr1[...]).astype(BF)
+        go(wa.at[:, xm], wr2, wxs.at[3], wxr.at[3], west)
+
+    def w_x2():
+        came(wl2, wxs.at[2], wxr.at[2])
+        came(wr2, wxs.at[3], wxr.at[3])
+        wb[...] = add(wa[:, x], wl2[...], wr2[...]).astype(BF)
+        go(wb.at[y2, :, 0:1280], vl1, wys.at[0], wyr.at[0], up)
+        go(wb.at[y2, :, 1280:2560], vr1, wys.at[1], wyr.at[1], down)
+
+    def w_y():
+        came(vl1, wys.at[0], wyr.at[0])
+        wb[yp, :, 0:1280] = add(wb[yp, :, 0:1280], vl1[...]).astype(BF)
+        go(wb.at[yp], vl2, wys.at[2], wyr.at[2], up)
+        came(vr1, wys.at[1], wyr.at[1])
+        wb[ym, :, 1280:2560] = add(wb[ym, :, 1280:2560], vr1[...]).astype(BF)
+        go(wb.at[ym], vr2, wys.at[3], wyr.at[3], down)
+
+    def w_y2():
+        came(vl2, wys.at[2], wyr.at[2])
+        came(vr2, wys.at[3], wyr.at[3])
+        summed = add(wb[y], vl2[...], vr2[...]).astype(BF)
+        for j in range(NZ):
+            wc[j, 0] = summed[:, j * 128:(j + 1) * 128]
+            c = 16 + j // 4
+            wc[j, 1] = summed[:, c * 128:(c + 1) * 128]
+        for o in FAR_FIRST:
+            zz = ring[o]
+            go(wc.at[zz], wz.at[o - 1], wzs.at[o - 1], wzr.at[o - 1], at(zz, x, y, k))
+
+    def w_z():
+        total = wc[z].astype(F32)
+        for o in range(1, NZ):
+            came(wz.at[o - 1], wzs.at[o - 1], wzr.at[o - 1])
+            total = total + wz[o - 1].astype(F32)
+        wd[z] = total.astype(BF)
+        for o in FAR_FIRST:
+            go(wd.at[z], wd.at[z], wgs.at[o - 1], wgr.at[o - 1], at(ring[o], x, y, k))
+
+    def w_z2():
+        for o in range(1, NZ):
+            came(wd.at[(z + NZ - o) % NZ], wgs.at[o - 1], wgr.at[o - 1])
+        for j in range(16):
+            we[x, :, j * 128:(j + 1) * 128] = wd[j, 0]
+        for c in range(4):
+            we[x, :, 2048 + c * 128:2048 + (c + 1) * 128] = wd[4 * c, 1]
+        go(we.at[x], we.at[x], wes.at[0], wer.at[0], east)
+        go(we.at[x], we.at[x], wes.at[1], wer.at[1], west)
+
+    def w_x3():
+        came(we.at[xm], wes.at[0], wer.at[0])
+        part = we.at[xm, :, 0:1280]
+        go(part, part, wes.at[2], wer.at[2], east)
+        came(we.at[xp], wes.at[1], wer.at[1])
+        part = we.at[xp, :, 1280:2560]
+        go(part, part, wes.at[3], wer.at[3], west)
+
+    def w_end():
+        came(we.at[x2, :, 0:1280], wes.at[2], wer.at[2])
+        came(we.at[x2, :, 1280:2560], wes.at[3], wer.at[3])
+        for i in range(NX):
+            total = we[i].astype(F32) * grad_scale
+            win_out[i * 16:(i + 1) * 16, :] = total[:, :2048]
+            wout_out[i * 16:(i + 1) * 16, :] = total[:, 2048:]
+
     own.wait()
+    for i, source in enumerate((x2, xm, xp)):
+        came(gx.at[source], gs.at[i], gr.at[i])
+    compute(0)
+    w_core()
+    t_core(0)
+    compute(1)
+    w_x()
+    t_y(0)
+    t_core(1)
+    compute(2)
+    w_x2()
+    t_z(0)
+    t_y(1)
+    t_core(2)
+    compute(3)
+    w_y()
+    t_z(1)
+    t_y(2)
+    t_core(3)
+    w_y2()
+    t_z(2)
+    t_y(3)
+    w_z()
+    t_z(3)
+    t_z2()
+    w_z2()
+    w_x3()
+    t_end()
+    w_end()
     for copy in sent:
         copy.wait_send()
 
 
-def reduce_all(part, wg):
+def back(grads, rows, wg, table_scale, grad_scale):
     v = pltpu.VMEM
     return pl.pallas_call(
-        reduce_kernel,
-        name="reduce_all",
+        functools.partial(back_kernel, table_scale, grad_scale),
+        name="back",
         out_shape=(
             jax.ShapeDtypeStruct((128, COLS), F32),
-            jax.ShapeDtypeStruct((NX, 16, 2560), F32),
+            jax.ShapeDtypeStruct((64, 2048), F32),
+            jax.ShapeDtypeStruct((64, 512), F32),
         ),
-        in_specs=[ANY, ANY],
-        out_specs=(VM, VM),
+        in_specs=[VM] * 3,
+        out_specs=(VM,) * 3,
         scratch_shapes=[
+            v((NX, 256, COLS), BF), v((4, 4, NY, 128, COLS), BF),
             v((4, 4, NY, 128, COLS), BF), v((4, 4, NY, 128, COLS), BF),
             v((4, 4, 64, COLS), BF), v((4, 4, 64, COLS), BF),
             v((4, 4, 128, COLS), BF), v((4, 4, 128, COLS), BF),
-            v((4, 4, 128, COLS), BF), v((15, 128, COLS), BF),
+            v((4, 4, 128, COLS), BF), v((3, 4, 128, COLS), BF),
+            v((4, 128, COLS), BF), v((3, 128, COLS), BF),
             v((NY, NX, 16, 2560), BF), v((NY, NX, 16, 2560), BF),
             v((2, 16, 2560), BF), v((2, 16, 2560), BF),
             v((4, 16, 2560), BF), v((4, 16, 2560), BF), v((4, 16, 2560), BF),
             v((16, 1280), BF), v((16, 1280), BF), v((16, 2560), BF), v((16, 2560), BF),
-            v((20, 16, 128), BF), v((15, 16, 128), BF), v((15, 16, 128), BF),
-            v((16, 16, 128), F32), v((16, 16, 128), F32), v((16, 2560), F32),
-            DMA((4,)), DMA((4,)), DMA((4, 4)), DMA((4, 4)), DMA((15,)), DMA((15,)), DMA((3,)),
+            v((NZ, 2, 16, 128), BF), v((15, 2, 16, 128), BF),
+            v((NZ, 2, 16, 128), BF), v((NX, 16, 2560), BF),
+            DMA((3,)), DMA((3,)),
+            DMA((4,)), DMA((4,)), DMA((4, 4)), DMA((4, 4)), DMA((3,)), DMA((3,)),
+            DMA((3,)), DMA((3,)), DMA((2,)),
             DMA, DMA, DMA((4,)), DMA((4,)), DMA((4,)), DMA((4,)),
-            DMA((15, 2)), DMA((15, 2)), DMA((15, 2)), DMA((15, 2)), DMA((3,)), DMA((3,)),
+            DMA((15,)), DMA((15,)), DMA((15,)), DMA((15,)), DMA((4,)), DMA((4,)),
         ],
         compiler_params=pltpu.CompilerParams(
             collective_id=3, has_side_effects=True, vmem_limit_bytes=VMEM_LIMIT
         ),
-    )(part, wg)
+    )(grads, rows, wg)
 
 
 def silu_grad(argument):
@@ -549,7 +598,7 @@
     return lax.dot_general(a, b, (((ca,), (cb,)), ((), ())), preferred_element_type=F32)
 
 
-def layer_kernel(lengths, rows, cot, w_in, w_out, out, grad, pin, pout, act, proj, att, gh):
+def layer_kernel(lengths, rows, cot, w_in, w_out, out, grad, wg, act, proj, att, gh):
     width = D // HEADS
     scale = width ** (-0.5)
     values = rows[...].astype(F32)
@@ -581,7 +630,7 @@
     mixed = (normed_out * gate).astype(BF)
     out[...] = (values + dot(mixed, w_out[...], 1, 0)).astype(BF)
     cotangent = cot[...]
-    pout[...] = dot(mixed, cotangent, 0, 0).astype(BF)
+    wg[:, 4 * D:] = dot(mixed, cotangent, 0, 0).astype(BF)
     grad_mixed = dot(cotangent, w_out[...], 1, 1)
     att[...] = norm_back(grad_mixed * gate, normed_out, out_inverse)
     gh[:, :D] = (grad_mixed * normed_out * silu_grad(proj[:, :D])).astype(BF)
@@ -602,7 +651,7 @@
                 c = slice(D + p * D + h * width, D + p * D + (h + 1) * width)
                 gh[r, c] = (parts[p] * silu_grad(proj[r, c])).astype(BF)
     grad_projected = gh[...]
-    pin[...] = dot(half_in, grad_projected, 0, 0).astype(BF)
+    wg[:, :4 * D] = dot(half_in, grad_projected, 0, 0).astype(BF)
     grad_normed = dot(grad_projected, w_in[...], 1, 1)
     grad[...] = (
         cotangent.astype(F32) + norm_back(grad_normed, normed_in, in_inverse)
@@ -617,11 +666,10 @@
         out_shape=(
             jax.ShapeDtypeStruct((256, D), BF),
             jax.ShapeDtypeStruct((256, D), BF),
-            jax.ShapeDtypeStruct((D, 4 * D), BF),
-            jax.ShapeDtypeStruct((D, D), BF),
+            jax.ShapeDtypeStruct((D, 5 * D), BF),
         ),
         in_specs=[pl.BlockSpec(memory_space=pltpu.SMEM)] + [VM] * 4,
-        out_specs=(VM,) * 4,
+        out_specs=(VM,) * 3,
         scratch_shapes=[
             v((256, 3 * D), BF), v((256, 4 * D), F32), v((256, D), F32), v((256, 4 * D), BF),
         ],
@@ -673,25 +721,20 @@
     my_lengths = jnp.sum(jnp.where(xs[:, None] == x, proc_lengths, 0), axis=0)
 
     id_flat = id_all.reshape(64, TABLES, SLOT)
-    looked = lookup(sel, id_flat, tabs.reshape(TABLES, DISTINCT, COLS))
-    rows = exchange(looked.reshape(NX, 256, COLS), True)
-    forward_out, grad_rows, partial_in, partial_out = layer(
+    looked, id_rows = lookup(sel, id_flat, tabs.reshape(TABLES, DISTINCT, COLS))
+    rows = exchange(looked.reshape(NX, 256, COLS))
+    forward_out, grad_rows, wg = layer(
         my_lengths, rows, cotangent[0], w_in.reshape(D, 4 * D), w_out.reshape(D, D)
     )
-    columns = exchange(grad_rows, False)
-    part = scatter(sel, id_flat, columns.reshape(1024, COLS))
-    wg = jnp.concatenate([partial_in, partial_out], axis=1).reshape(NY, 2, NX, 16, 2560)
-    table_sum, weight_sum = reduce_all(part.reshape(4, 4, NY, 2, 128, COLS), wg)
     events = NB * item_ids.shape[1]
-    table_scale = (DISTINCT / events) ** 0.5
-    grad_scale = events ** (-0.5)
-    weight_sum = weight_sum.reshape(64, 2560)
-    return (
-        forward_out[None],
-        (table_sum * table_scale)[None],
-        weight_sum[:, :2048] * grad_scale,
-        weight_sum[:, 2048:] * grad_scale,
+    table_grad, grad_in, grad_out = back(
+        grad_rows,
+        id_rows,
+        wg.reshape(NY, 2, NX, 16, 2560),
+        (DISTINCT / events) ** 0.5,
+        events ** (-0.5),
     )
+    return forward_out[None], table_grad[None], grad_in, grad_out
 
 
 def solution(mesh):

time: 221 us -> 171 us (0.77); the launches traced: 217 us -> 170 us
  Pallas kernels: 202 us -> 159 us
  other arithmetic: 10.4 us -> 1.98 us
  local copies, waits for them, and re-layouts: 3.77 us -> 8.68 us
    pallas_call x5 -> x3, Pallas kernels: 140 us -> 96 us  [the longest x1 68.6 us: back(): pl.pallas_call(functools.partial(back_kernel, table_scale, grad_scale), n...]
    unnamed x5 -> x8, local copies, waits for them, and re-layouts: 0.86 us -> 5.77 us
    concatenate x1 -> x0, other arithmetic: 3.5 us -> none  [on_device(): jnp.concatenate([partial_in, partial_out], axis=1)]
    mul x2 -> x0, other arithmetic: 3.45 us -> none  [the longest x1 1.88 us: on_device(): weight_sum[:, :2048] * grad_scale]
where the time goes in v2:
time: 171 us; the launch traced here: 170 us
  Pallas kernels  159 us (93%)
  local copies, waits for them, and re-layouts  8.68 us (5%)
  other arithmetic  1.98 us (1%)
    pallas_call x1, Pallas kernels, back(): pl.pallas_call(functools.partial(back_kernel, table_scale, grad_scale), n...  68.6 us
    pallas_call x1, Pallas kernels, gather_all(): pl.pallas_call(gather_kernel, name='gather_all', out_shape=(jax.ShapeDtyp...  49.9 us
    pallas_call x1, Pallas kernels, lookup(): pl.pallas_call(lookup_kernel, name='lookup', out_shape=(jax.ShapeDtypeStr...  17.4 us
    pallas_call x1, Pallas kernels, layer(): pl.pallas_call(layer_kernel, name='layer', out_shape=(jax.ShapeDtypeStruc...  12.9 us
    pallas_call x1, Pallas kernels, exchange(): pl.pallas_call(exchange_kernel, name='exchange_rows', out_shape=jax.Shape...  10 us
    unnamed x8, local copies, waits for them, and re-layouts  5.77 us

profile of v2, /device:TPU:6, one launch (start us, length us, event | category | flops | bytes accessed | tf_op | source)
XLA Modules:
  0.0 170.2 jit_solution(13654590501235723973)
XLA Ops:
  0.6 0.0 copy-start
  0.7 0.8 copy.18
  1.5 0.1 reshape.123
  1.6 0.7 pad_add_fusion
  2.4 0.6 broadcast_in_dim.89.meta
  3.0 0.0 copy-done
  3.0 0.6 copy.23
  3.6 49.9 %gather_all.1 = (bf16[16,4,2,128,128]{4,3,2,1,0:T(8,128)(2,1)}, bf16[4,2,4,16,2048]{4,3,2,1,0:T(8,128)(2,1)}, bf16[4,2,4,16,512]{4,3,2,1,0:T(8,128)(2,1)}, s32[4,2,8,16,128]{4,3,2,1,0:T(8,128)}, s32[4,8,128]{2,1,0:T(8,128)}) custom-call(bf16[4,2,128,128]{3,2,1,0:T(8,128)(2,1)} %bitcast.40, bf16[4,16,2048]{2,1,0:T(8,128)(2,1)} %bitcast.41, ...), custom_call_target="tpu_custom_call" | custom-call | tf_op jit(solution)/shard_map/gather_all/pallas_call | solution.py:204
  53.6 0.7 slice.12
  54.3 0.2 select_reduce_fusion.4
  54.5 0.1 iota_compare_fusion
  54.6 0.1 broadcast_and_fusion
  54.7 0.1 and.34
  54.8 0.1 select_reduce_fusion.2
  54.9 0.1 copy.19
  55.0 0.1 select_reduce_fusion
  55.1 0.6 add_select_fusion
  55.7 0.1 copy.20
  55.8 0.6 select_n.61.sel
  56.4 17.4 %lookup.1 = (bf16[1024,128]{1,0:T(8,128)(2,1)}, s32[16,1024]{1,0:T(8,128)}) custom-call(s32[8]{0:T(128)} %select_n.61.sel, s32[64,16,128]{2,1,0:T(8,128)} %bitcast.27, s32[64,16,128]{2,1,0:T(8,128)} %bitcast.28, s32[64,16,128]{2,1,0:T(8,128)} %bitcast.29, s32[64,16,128]{2,1,0:T(8,128)} %bitcast.30, s32[64,16,128]{2,1,0:T(8,128)} %bitcast.31, ...), custom_call_target="tpu_custom_call" | custom-call | tf_op jit(solution)/shard_map/lookup/pallas_call | solution.py:257
  73.8 10.0 %exchange_rows.1.rows = bf16[256,512]{1,0:T(8,128)(2,1)} custom-call(bf16[4,256,128]{2,1,0:T(8,128)(2,1)} %bitcast.42), custom_call_target="tpu_custom_call" | custom-call | tf_op jit(solution)/shard_map/exchange_rows/pallas_call | solution.py:306
  83.8 12.9 %layer.1 = (bf16[256,512]{1,0:T(8,128)(2,1)}, bf16[256,512]{1,0:T(8,128)(2,1)}, bf16[512,2560]{1,0:T(8,128)(2,1)}) custom-call(s32[2]{0:T(128)} %get-tuple-element.37.lengths, bf16[256,512]{1,0:T(8,128)(2,1)} %exchange_rows.1.rows, bf16[256,512]{1,0:T(8,128)(2,1)} %bitcast.44, bf16[512,2048]{1,0:T(8,128)(2,1)} %bitcast.37, bf16[512,512]{1,0:T(8,128)(2,1)} %bitcast.38), custom_call_target="tpu_custom_call" | custom-call | tf_op jit(solution)/shard_map/layer/pallas_call | solution.py:663
  96.7 68.6 %back.1 = (f32[128,128]{1,0:T(8,128)}, f32[64,2048]{1,0:T(8,128)}, f32[64,512]{1,0:T(8,128)}) custom-call(bf16[256,512]{1,0:T(8,128)(2,1)} %get-tuple-element.24.grads, s32[16,1024]{1,0:T(8,128)} %get-tuple-element.25.rows, bf16[4,2,4,16,2560]{4,3,2,1,0:T(8,128)(2,1)} %bitcast.36), custom_call_target="tpu_custom_call" | custom-call | tf_op jit(solution)/shard_map/back/pallas_call | solution.py:544
  165.3 1.5 copy.27
  166.8 1.9 %copy.28 = f32[64,2048]{1,0:T(8,128)} copy(f32[64,2048]{1,0:T(8,128)} %get-tuple-element.46) | data formatting | bytes 1048576
  168.6 1.6 copy.29
  (6 shorter events, 0.0 us)
Async XLA Ops:
  0.6 2.3 %copy-start = (s32[1,16384,16]{1,2,0:T(8,128)S(1)}, s32[1,16384,16]{1,2,0:T(8,128)}, u32[]{:S(2)}) copy-start(s32[1,16384,16]{1,2,0:T(8,128)} %param.8) | copy-start | bytes 3145732

commit v3 on v2

--- a/solution.py
+++ b/solution.py
@@ -57,22 +57,30 @@
 DMA = pltpu.SemaphoreType.DMA
 
 
-Z_SLICES = [(d, s) for s in range(1, 9) for d in (-1, 1) if d < 0 or s < 8]
-Z_INDEX = {pair: i for i, pair in enumerate(Z_SLICES)}
-
-
-def gather_kernel(
-    tab, win, wout, ids, meta, tabs, wfi, wfo, idall, metall,
-    zs, zr, ys, yr, cs, cr, ws, wr, os_, or_, is_, ir, ms, mr, loc,
+NEAR = (1, 15, 2)
+JUMPS = (4, 12, 8)
+ARRIVALS = [(0, r) for r in NEAR] + [(j, 0) for j in JUMPS] + [(j, r) for j in JUMPS for r in NEAR]
+INDEX = {pair: i for i, pair in enumerate(ARRIVALS)}
+
+
+def front_kernel(
+    tab, win, wout, ids, meta, out, id_rows, lens, wfi, wfo,
+    tabs, idall, metall, columns, total, looked,
+    zs, zr, ys, yr, cs, cr, ws, wr, os_, or_, is_, ir, ms, mr, es, er, loc,
 ):
     z, x, y, k = place()
-    right, left = at((z + 1) % NZ, x, y, k), at((z + NZ - 1) % NZ, x, y, k)
-    yp, ym, y2 = (y + 1) % NY, (y + 3) % NY, (y + 2) % NY
-    up, down = at(z, x, yp, k), at(z, x, ym, k)
-    xp, xm, x2 = (x + 1) % NX, (x + 3) % NX, (x + 2) % NX
-    east, west, far = at(z, xp, y, k), at(z, xm, y, k), at(z, x2, y, k)
+    bal = y * 2 + k
+    y_peers = [(y + 1) % NY, (y + 3) % NY, (y + 2) % NY]
+    x_peers = [(x + 1) % NX, (x + 3) % NX, (x + 2) % NX]
+    y_from = [y_peers[1], y_peers[0], y_peers[2]]
+    x_from = [x_peers[1], x_peers[0], x_peers[2]]
+    y_devices = [at(z, x, peer, k) for peer in y_peers]
+    x_devices = [at(z, peer, y, k) for peer in x_peers]
     other = at(z, x, y, 1 - k)
-    greet([right, left, up, down, east, west, far, other])
+    offsets = NEAR + JUMPS
+    z_devices = {o: at((z + o) % NZ, x, y, k) for o in offsets}
+    z_sources = [at((z + NZ - o) % NZ, x, y, k) for o in (2, )]
+    greet(list(z_devices.values()) + z_sources + y_devices + x_devices + [other])
 
     sent = []
 
@@ -81,237 +89,203 @@
         copy.start()
         sent.append(copy)
 
-    def came(dst, send, recv, device):
-        rcopy(dst, dst, send, recv, device).wait_recv()
-
+    def came(dst, send, recv):
+        rcopy(dst, dst, send, recv, other).wait_recv()
+
+    def origin(pair):
+        return (z + 2 * NZ - pair[0] - pair[1]) % NZ
+
+    for o in JUMPS:
+        i = INDEX[(o, 0)]
+        go(tab.at[y, k], tabs.at[z, y, k], zs.at[i], zr.at[i], z_devices[o])
+    for o in NEAR:
+        i = INDEX[(0, o)]
+        go(tab.at[y, k], tabs.at[z, y, k], zs.at[i], zr.at[i], z_devices[o])
+    for i in range(3):
+        go(ids, idall.at[y, k], is_.at[i], ir.at[i], y_devices[i])
+        go(meta, metall.at[x], ms.at[i], mr.at[i], x_devices[i])
+    for i in range(3):
+        go(win.at[x], wfi.at[y, k, x], ws.at[i], wr.at[i], y_devices[i])
+        go(wout.at[x], wfo.at[y, k, x], os_.at[i], or_.at[i], y_devices[i])
     local = [
-        pltpu.make_async_copy(tab, tabs.at[z], loc.at[0]),
-        pltpu.make_async_copy(win.at[x], wfi.at[y, k, x], loc.at[1]),
-        pltpu.make_async_copy(wout.at[x], wfo.at[y, k, x], loc.at[2]),
-        pltpu.make_async_copy(ids, idall.at[y, k], loc.at[3]),
-        pltpu.make_async_copy(meta, metall.at[x], loc.at[4]),
+        pltpu.make_async_copy(win.at[x], wfi.at[y, k, x], loc.at[0]),
+        pltpu.make_async_copy(wout.at[x], wfo.at[y, k, x], loc.at[1]),
+        pltpu.make_async_copy(ids, idall.at[y, k], loc.at[2]),
+        pltpu.make_async_copy(meta, metall.at[x], loc.at[3]),
     ]
-    go(tab.at[y, k], tabs.at[z, y, k], zs.at[0], zr.at[0], right)
-    go(tab.at[y, k], tabs.at[z, y, k], zs.at[1], zr.at[1], left)
     for copy in local:
         copy.start()
-    for i, (peer, dev) in enumerate(((xp, east), (xm, west), (x2, far))):
-        go(meta, metall.at[x], ms.at[i], mr.at[i], dev)
-    go(ids, idall.at[y, k], is_.at[0], ir.at[0], up)
-    go(ids, idall.at[y, k], is_.at[1], ir.at[1], down)
-    go(win.at[x], wfi.at[y, k, x], ws.at[0], wr.at[0], up)
-    go(win.at[x], wfi.at[y, k, x], ws.at[1], wr.at[1], down)
-    go(wout.at[x], wfo.at[y, k, x], os_.at[0], or_.at[0], up)
-    go(wout.at[x], wfo.at[y, k, x], os_.at[1], or_.at[1], down)
-
-    def slot(d, s):
-        return (z + d * s + NZ) % NZ
-
-    def weights_y_relay():
-        came(idall.at[ym, k], is_.at[0], ir.at[0], up)
-        go(idall.at[ym, k, 0:4], idall.at[ym, k, 0:4], is_.at[2], ir.at[2], up)
-        came(idall.at[yp, k], is_.at[1], ir.at[1], down)
-        go(idall.at[yp, k, 4:8], idall.at[yp, k, 4:8], is_.at[3], ir.at[3], down)
-        for full, s_, r_, half in ((wfi, ws, wr, 1024), (wfo, os_, or_, 256)):
-            came(full.at[ym, k, x], s_.at[0], r_.at[0], up)
-            part = full.at[ym, k, x, :, 0:half]
-            go(part, part, s_.at[2], r_.at[2], up)
-            came(full.at[yp, k, x], s_.at[1], r_.at[1], down)
-            part = full.at[yp, k, x, :, half:2 * half]
-            go(part, part, s_.at[3], r_.at[3], down)
-
-    def weights_x_send():
-        came(idall.at[y2, k, 0:4], is_.at[2], ir.at[2], up)
-        came(idall.at[y2, k, 4:8], is_.at[3], ir.at[3], down)
+
+    def from_z(pair):
+        i, zz = INDEX[pair], origin(pair)
+        mine = tabs.at[zz, y, k]
+        came(mine, zs.at[i], zr.at[i])
+        if pair[1] == 0:
+            for r in NEAR:
+                j = INDEX[(pair[0], r)]
+                go(mine, mine, zs.at[j], zr.at[j], z_devices[r])
+        for p in range(3):
+            go(mine, mine, ys.at[i, p], yr.at[i, p], y_devices[p])
+
+    def from_y(pair):
+        i, zz = INDEX[pair], origin(pair)
+        for p in range(3):
+            came(tabs.at[zz, y_from[p], k], ys.at[i, p], yr.at[i, p])
+        go(tabs.at[zz, :, k], tabs.at[zz, :, k], cs.at[i], cr.at[i], other)
+
+    def from_core(pair):
+        i, zz = INDEX[pair], origin(pair)
+        came(tabs.at[zz, :, 1 - k], cs.at[i], cr.at[i])
+
+    lane = lax.broadcasted_iota(jnp.int32, (8 * SLOT, TABLES), 1)
+    vocab = lax.broadcasted_iota(jnp.int32, (8 * SLOT, 256), 1)
+
+    def sum_table(t, read):
+        picked = jnp.sum(jnp.where(lane == t, columns[...], 0), axis=1, keepdims=True)
+
+        def body(part, carry):
+            hot = jnp.where(picked - part * 256 == vocab, 1.0, 0.0).astype(BF)
+            total[...] += jnp.dot(hot, read(part), preferred_element_type=F32)
+            return carry
+
+        lax.fori_loop(0, 4, body, 0)
+
+    def read_own(part):
+        return tab[part].reshape(256, COLS)
+
+    def choose_ids():
+        for i in range(3):
+            came(metall.at[x_from[i]], ms.at[i], mr.at[i])
         local[3].wait()
-        go(idall.at[:, k], idall.at[:, k], is_.at[4], ir.at[4], other)
+        came(idall.at[:, 1 - k], is_.at[3], ir.at[3])
+        for xx in range(NX):
+            mine = jnp.zeros((1, SLOT), jnp.int32)
+            moved = jnp.zeros((TABLES, SLOT), jnp.int32)
+            for b in range(NB):
+                surplus = metall[xx, 16 + b:17 + b, :]
+                is_mine = jnp.where(bal == b, 1, 0)
+                mine = mine + surplus * is_mine
+                sends = jnp.where(metall[xx, 24 + b:25 + b, :] == bal, 1, 0)
+                first = idall[b // 2, b % 2, 2 * xx]
+                second = idall[b // 2, b % 2, 2 * xx + 1]
+                moved = moved + sends * (first + surplus * (second - first))
+            for s in range(NSEQ):
+                away = mine if s == 1 else 1 - mine
+                kept = idall[y, k, 2 * xx + s]
+                chosen = kept + away * (moved - kept)
+                i = 2 * xx + s
+                id_rows[:, i * SLOT:(i + 1) * SLOT] = chosen
+                columns[i * SLOT:(i + 1) * SLOT, :] = jnp.transpose(chosen)
+        mine = jnp.zeros((1, SLOT), jnp.int32)
+        moved = jnp.zeros((1, SLOT), jnp.int32)
+        kept = [jnp.zeros((1, SLOT), jnp.int32) for _ in range(NSEQ)]
+        for b in range(NB):
+            surplus = metall[x, 16 + b:17 + b, :]
+            is_mine = jnp.where(bal == b, 1, 0)
+            mine = mine + surplus * is_mine
+            sends = jnp.where(metall[x, 24 + b:25 + b, :] == bal, 1, 0)
+            first = metall[x, 2 * b:2 * b + 1, :]
+            second = metall[x, 2 * b + 1:2 * b + 2, :]
+            moved = moved + sends * (first + surplus * (second - first))
+            kept[0] = kept[0] + is_mine * first
+            kept[1] = kept[1] + is_mine * second
+        lens[...] = jnp.zeros_like(lens)
+        lens[0:1, :] = kept[0] + (1 - mine) * (moved - kept[0])
+        lens[1:2, :] = kept[1] + mine * (moved - kept[1])
+
+    def ids_core():
+        local[2].wait()
+        for i in range(3):
+            came(idall.at[y_from[i], k], is_.at[i], ir.at[i])
+        go(idall.at[:, k], idall.at[:, k], is_.at[3], ir.at[3], other)
+
+    def weights_x():
+        local[0].wait()
         local[1].wait()
-        local[2].wait()
-        for full, s_, r_, half in ((wfi, ws, wr, 1024), (wfo, os_, or_, 256)):
-            came(full.at[y2, k, x, :, 0:half], s_.at[2], r_.at[2], up)
-            came(full.at[y2, k, x, :, half:2 * half], s_.at[3], r_.at[3], down)
-            go(full.at[:, k, x], full.at[:, k, x], s_.at[4], r_.at[4], east)
-            go(full.at[:, k, x], full.at[:, k, x], s_.at[5], r_.at[5], west)
-
-    def weights_x_relay():
         for full, s_, r_ in ((wfi, ws, wr), (wfo, os_, or_)):
-            came(full.at[:, k, xm], s_.at[4], r_.at[4], east)
-            part = full.at[0:2, k, xm]
-            go(part, part, s_.at[6], r_.at[6], east)
-            came(full.at[:, k, xp], s_.at[5], r_.at[5], west)
-            part = full.at[2:4, k, xp]
-            go(part, part, s_.at[7], r_.at[7], west)
+            for i in range(3):
+                came(full.at[y_from[i], k, x], s_.at[i], r_.at[i])
+            for i in range(3):
+                part = full.at[:, k, x]
+                go(part, part, s_.at[3 + i], r_.at[3 + i], x_devices[i])
 
     def weights_core():
         for full, s_, r_ in ((wfi, ws, wr), (wfo, os_, or_)):
-            came(full.at[0:2, k, x2], s_.at[6], r_.at[6], east)
-            came(full.at[2:4, k, x2], s_.at[7], r_.at[7], west)
-            go(full.at[:, k], full.at[:, k], s_.at[8], r_.at[8], other)
-
-    for st in range(1, 11):
-        for d in (-1, 1):
-            if (d, st) not in Z_INDEX:
-                continue
-            i, zz = Z_INDEX[(d, st)], slot(d, st)
-            mine = tabs.at[zz, y, k]
-            onward = right if d < 0 else left
-            came(mine, zs.at[i], zr.at[i], onward)
-            if (d, st + 1) in Z_INDEX:
-                j = Z_INDEX[(d, st + 1)]
-                go(mine, mine, zs.at[j], zr.at[j], onward)
-            go(mine, mine, ys.at[i, 0], yr.at[i, 0], up)
-            go(mine, mine, ys.at[i, 1], yr.at[i, 1], down)
-        for d in (-1, 1):
-            if (d, st - 1) not in Z_INDEX:
-                continue
-            i, zz = Z_INDEX[(d, st - 1)], slot(d, st - 1)
-            came(tabs.at[zz, ym, k], ys.at[i, 0], yr.at[i, 0], up)
-            part = tabs.at[zz, ym, k, 0:64]
-            go(part, part, ys.at[i, 2], yr.at[i, 2], up)
-            came(tabs.at[zz, yp, k], ys.at[i, 1], yr.at[i, 1], down)
-            part = tabs.at[zz, yp, k, 64:128]
-            go(part, part, ys.at[i, 3], yr.at[i, 3], down)
-        for d in (-1, 1):
-            if (d, st - 2) not in Z_INDEX:
-                continue
-            i, zz = Z_INDEX[(d, st - 2)], slot(d, st - 2)
-            came(tabs.at[zz, y2, k, 0:64], ys.at[i, 2], yr.at[i, 2], up)
-            came(tabs.at[zz, y2, k, 64:128], ys.at[i, 3], yr.at[i, 3], down)
-            go(tabs.at[zz, :, k], tabs.at[zz, :, k], cs.at[i], cr.at[i], other)
-        if st == 1:
-            weights_y_relay()
-        if st == 2:
-            weights_x_send()
-        if st == 5:
-            weights_x_relay()
-        if st == 8:
+            for i in range(3):
+                came(full.at[:, k, x_from[i]], s_.at[3 + i], r_.at[3 + i])
+            go(full.at[:, k], full.at[:, k], s_.at[6], r_.at[6], other)
+
+    total[...] = jnp.zeros_like(total)
+    for pair in ARRIVALS[:3]:
+        from_z(pair)
+    ids_core()
+    for pair in ARRIVALS[3:6]:
+        from_z(pair)
+    choose_ids()
+    sum_table(z, read_own)
+    weights_x()
+    for pair in ARRIVALS[6:9]:
+        from_z(pair)
+    from_y(ARRIVALS[0])
+    for n in range(15):
+        if n < 3:
+            for pair in ARRIVALS[9 + 2 * n:11 + 2 * n]:
+                from_z(pair)
+        if n < 14:
+            from_y(ARRIVALS[n + 1])
+        if n == 13:
             weights_core()
-
-    for i, peer in enumerate((xm, xp, x2)):
-        came(metall.at[peer], ms.at[i], mr.at[i], other)
-    came(idall.at[:, 1 - k], is_.at[4], ir.at[4], other)
-    came(wfi.at[:, 1 - k], ws.at[8], wr.at[8], other)
-    came(wfo.at[:, 1 - k], os_.at[8], or_.at[8], other)
-    for (d, s), i in Z_INDEX.items():
-        came(tabs.at[slot(d, s), :, 1 - k], cs.at[i], cr.at[i], other)
+        from_core(ARRIVALS[n])
+        zz = origin(ARRIVALS[n])
+        sum_table(zz, lambda part, zz=zz: tabs[zz, part].reshape(256, COLS))
+
+    looked[...] = total[...].astype(BF).reshape(NX, 256, COLS)
+
+    def piece(i):
+        return out.at[:, pl.ds(pl.multiple_of(i * COLS, COLS), COLS)]
+
+    for i in (2, 0, 1):
+        go(looked.at[x_peers[i]], piece(x), es.at[i], er.at[i], x_devices[i])
+    own = pltpu.make_async_copy(looked.at[x], piece(x), loc.at[4])
+    own.start()
+    came(wfi.at[:, 1 - k], ws.at[6], wr.at[6])
+    came(wfo.at[:, 1 - k], os_.at[6], or_.at[6])
+    for i in range(3):
+        came(piece(x_from[i]), es.at[i], er.at[i])
+    own.wait()
     for copy in sent:
         copy.wait_send()
-    local[0].wait()
-    local[4].wait()
-
-
-def gather_all(tab, win, wout, ids, meta):
+
+
+def front(tab, win, wout, ids, meta):
+    v = pltpu.VMEM
     return pl.pallas_call(
-        gather_kernel,
-        name="gather_all",
+        front_kernel,
+        name="front",
         out_shape=(
-            jax.ShapeDtypeStruct((NZ, NY, 2, 128, COLS), BF),
+            jax.ShapeDtypeStruct((256, D), BF),
+            jax.ShapeDtypeStruct((TABLES, 8 * SLOT), jnp.int32),
+            jax.ShapeDtypeStruct((8, SLOT), jnp.int32),
             jax.ShapeDtypeStruct((NY, 2, NX, 16, 2048), BF),
             jax.ShapeDtypeStruct((NY, 2, NX, 16, 512), BF),
-            jax.ShapeDtypeStruct((NY, 2, 8, TABLES, SLOT), jnp.int32),
-            jax.ShapeDtypeStruct((NX, 8, 128), jnp.int32),
         ),
         in_specs=[VM] * 5,
-        out_specs=(ANY,) * 5,
+        out_specs=(VM, VM, VM, ANY, ANY),
         scratch_shapes=[
-            DMA((15,)), DMA((15,)), DMA((15, 4)), DMA((15, 4)), DMA((15,)), DMA((15,)),
-            DMA((9,)), DMA((9,)), DMA((9,)), DMA((9,)), DMA((5,)), DMA((5,)),
-            DMA((3,)), DMA((3,)), DMA((5,)),
+            v((NZ, NY, 2, 128, COLS), BF),
+            v((NY, 2, 8, TABLES, SLOT), jnp.int32),
+            v((NX, 32, 128), jnp.int32),
+            v((8 * SLOT, TABLES), jnp.int32),
+            v((8 * SLOT, COLS), F32),
+            v((NX, 256, COLS), BF),
+            DMA((15,)), DMA((15,)), DMA((15, 3)), DMA((15, 3)), DMA((15,)), DMA((15,)),
+            DMA((7,)), DMA((7,)), DMA((7,)), DMA((7,)), DMA((4,)), DMA((4,)),
+            DMA((3,)), DMA((3,)), DMA((3,)), DMA((3,)), DMA((5,)),
         ],
-        compiler_params=pltpu.CompilerParams(collective_id=0, has_side_effects=True),
+        compiler_params=pltpu.CompilerParams(
+            collective_id=0, has_side_effects=True, vmem_limit_bytes=VMEM_LIMIT
+        ),
     )(tab, win, wout, ids, meta)
-
-
-def lookup_kernel(sel, *refs):
-    slots, (table, out, rows, columns, total) = refs[:8], refs[8:]
-    t = pl.program_id(0)
-
-    @pl.when(t == 0)
-    def _():
-        for i in range(8):
-            rows[:, i * SLOT:(i + 1) * SLOT] = slots[i][0]
-            columns[i * SLOT:(i + 1) * SLOT, :] = jnp.transpose(slots[i][0])
-        total[...] = jnp.zeros_like(total)
-
-    lane = lax.broadcasted_iota(jnp.int32, (8 * SLOT, TABLES), 1)
-    picked = jnp.sum(jnp.where(lane == t, columns[...], 0), axis=1, keepdims=True)
-    acc = total[...]
-    for part in range(4):
-        vocab = lax.broadcasted_iota(jnp.int32, (8 * SLOT, 256), 1) + part * 256
-        hot = jnp.where(picked == vocab, 1.0, 0.0).astype(BF)
-        acc = acc + jnp.dot(
-            hot, table[0, part * 256:(part + 1) * 256, :], preferred_element_type=F32
-        )
-    total[...] = acc
-
-    @pl.when(t == TABLES - 1)
-    def _():
-        out[...] = acc.astype(BF)
-
-
-def slot_spec(i):
-    return pl.BlockSpec((1, TABLES, SLOT), lambda t, sel: (sel[i], 0, 0))
-
-
-def lookup(sel, ids, tables):
-    return pl.pallas_call(
-        lookup_kernel,
-        name="lookup",
-        out_shape=(
-            jax.ShapeDtypeStruct((8 * SLOT, COLS), BF),
-            jax.ShapeDtypeStruct((TABLES, 8 * SLOT), jnp.int32),
-        ),
-        grid_spec=pltpu.PrefetchScalarGridSpec(
-            num_scalar_prefetch=1,
-            grid=(TABLES,),
-            in_specs=[slot_spec(i) for i in range(8)]
-            + [pl.BlockSpec((1, DISTINCT, COLS), lambda t, sel: (t, 0, 0))],
-            out_specs=(
-                pl.BlockSpec((8 * SLOT, COLS), lambda t, sel: (0, 0)),
-                pl.BlockSpec((TABLES, 8 * SLOT), lambda t, sel: (0, 0)),
-            ),
-            scratch_shapes=[
-                pltpu.VMEM((8 * SLOT, TABLES), jnp.int32),
-                pltpu.VMEM((8 * SLOT, COLS), F32),
-            ],
-        ),
-    )(sel, *([ids] * 8), tables)
-
-
-def exchange_kernel(src, out, send, recv, loc):
-    z, x, y, k = place()
-    peers = [(x + 1) % NX, (x + 3) % NX, (x + 2) % NX]
-    devices = [at(z, peer, y, k) for peer in peers]
-    greet(devices)
-
-    def piece(i):
-        return out.at[:, pl.ds(pl.multiple_of(i * COLS, COLS), COLS)]
-
-    copies = []
-    for i, (peer, device) in enumerate(zip(peers, devices)):
-        copy = rcopy(src.at[peer], piece(x), send.at[i], recv.at[i], device)
-        copy.start()
-        copies.append(copy)
-    own = pltpu.make_async_copy(src.at[x], piece(x), loc)
-    own.start()
-    for i, source in enumerate((peers[1], peers[0], peers[2])):
-        landed = piece(source)
-        rcopy(landed, landed, send.at[i], recv.at[i], devices[i]).wait_recv()
-    for copy in copies:
-        copy.wait_send()
-    own.wait()
-
-
-def exchange(array):
-    return pl.pallas_call(
-        exchange_kernel,
-        name="exchange_rows",
-        out_shape=jax.ShapeDtypeStruct((256, D), BF),
-        in_specs=[VM],
-        out_specs=VM,
-        scratch_shapes=[DMA((3,)), DMA((3,)), DMA],
-        compiler_params=pltpu.CompilerParams(collective_id=1, has_side_effects=True),
-    )(array)
 
 
 OFFSETS = (2, 1, -1, 0)
@@ -611,7 +585,9 @@
     act[...] = activated[:, D:].astype(BF)
     place_i = lax.broadcasted_iota(jnp.int32, (SLOT, SLOT), 0)
     place_j = lax.broadcasted_iota(jnp.int32, (SLOT, SLOT), 1)
-    masks = [(place_j <= place_i) & (place_i < lengths[s]) for s in range(NSEQ)]
+    masks = [
+        (place_j <= place_i) & (place_i < lengths[s:s + 1, :]) for s in range(NSEQ)
+    ]
 
     def heads(s, h):
         r = slice(s * SLOT, (s + 1) * SLOT)
@@ -668,7 +644,7 @@
             jax.ShapeDtypeStruct((256, D), BF),
             jax.ShapeDtypeStruct((D, 5 * D), BF),
         ),
-        in_specs=[pl.BlockSpec(memory_space=pltpu.SMEM)] + [VM] * 4,
+        in_specs=[VM] * 5,
         out_specs=(VM,) * 3,
         scratch_shapes=[
             v((256, 3 * D), BF), v((256, 4 * D), F32), v((256, D), F32), v((256, 4 * D), BF),
@@ -680,51 +656,22 @@
 def on_device(
     item_ids, seq_lengths, surplus_slot, helper_map, embed_tables, weight_in, weight_out, cotangent
 ):
-    z, x, y, k = place()
-    bal = lax.axis_index("bal")
+    z = lax.axis_index("emb") // NX
     near = lax.dynamic_slice_in_dim(item_ids[0], z * 1024, 1024, 0)
     ids = jnp.transpose(near.reshape(8, SLOT, TABLES), (0, 2, 1))
     meta = jnp.concatenate(
         [seq_lengths.reshape(16), surplus_slot.reshape(8), helper_map.reshape(8)]
     )
-    meta = jnp.broadcast_to(jnp.pad(meta, (0, 96))[None], (8, 128))
-    tabs, w_in, w_out, id_all, meta_all = gather_all(
+    meta = jnp.broadcast_to(meta[:, None], (32, 128))
+    rows, id_rows, lengths, w_in, w_out = front(
         embed_tables.reshape(NY, 2, 128, COLS),
         weight_in.reshape(NX, 16, 2048),
         weight_out.reshape(NX, 16, 512),
         ids,
         meta,
     )
-    facts = meta_all[:, 0, :32]
-    lengths = facts[:, :16].reshape(NX, NB, NSEQ)
-    surplus = facts[:, 16:24]
-    helper = facts[:, 24:32]
-    bals = jnp.arange(NB, dtype=jnp.int32)[None]
-    is_source = helper == bal
-    source = jnp.sum(jnp.where(is_source, bals, 0), axis=1)
-    source_slot = jnp.sum(jnp.where(is_source, surplus, 0), axis=1)
-    my_slot = jnp.sum(jnp.where(bals == bal, surplus, 0), axis=1)
-    slots = jnp.arange(NSEQ, dtype=jnp.int32)[None]
-    xs = jnp.arange(NX, dtype=jnp.int32)
-    moved = slots == my_slot[:, None]
-    sel = jnp.where(
-        moved, (source * 8 + xs * 2 + source_slot)[:, None], bal * 8 + xs[:, None] * 2 + slots
-    ).reshape(8)
-    own_lengths = jnp.sum(jnp.where((bals == bal)[:, :, None], lengths, 0), axis=1)
-    moved_length = jnp.sum(
-        jnp.where(
-            is_source[:, :, None] & (slots[None] == source_slot[:, None, None]), lengths, 0
-        ),
-        axis=(1, 2),
-    )
-    proc_lengths = jnp.where(moved, moved_length[:, None], own_lengths)
-    my_lengths = jnp.sum(jnp.where(xs[:, None] == x, proc_lengths, 0), axis=0)
-
-    id_flat = id_all.reshape(64, TABLES, SLOT)
-    looked, id_rows = lookup(sel, id_flat, tabs.reshape(TABLES, DISTINCT, COLS))
-    rows = exchange(looked.reshape(NX, 256, COLS))
     forward_out, grad_rows, wg = layer(
-        my_lengths, rows, cotangent[0], w_in.reshape(D, 4 * D), w_out.reshape(D, D)
+        lengths, rows, cotangent[0], w_in.reshape(D, 4 * D), w_out.reshape(D, D)
     )
     events = NB * item_ids.shape[1]
     table_grad, grad_in, grad_out = back(

time: 171 us -> 154 us (0.901)
  Pallas kernels: 159 us -> 145 us
    pallas_call x3 -> x1, Pallas kernels: 77.4 us -> 60.6 us  [front(): pl.pallas_call(front_kernel, name='front', out_shape=(jax.ShapeDtypeStruc...]
    pallas_call x1, Pallas kernels: 68.6 us -> 71.2 us  [back(): pl.pallas_call(functools.partial(back_kernel, table_scale, grad_scale), n...]
where the time goes in v3:
time: 154 us; the launch traced here: 153 us
  Pallas kernels  145 us (94%)
  local copies, waits for them, and re-layouts  7.18 us (5%)
    pallas_call x1, Pallas kernels, back(): pl.pallas_call(functools.partial(back_kernel, table_scale, grad_scale), n...  71.2 us
    pallas_call x1, Pallas kernels, front(): pl.pallas_call(front_kernel, name='front', out_shape=(jax.ShapeDtypeStruc...  60.6 us
    pallas_call x1, Pallas kernels, layer(): pl.pallas_call(layer_kernel, name='layer', out_shape=(jax.ShapeDtypeStruc...  12.9 us
    unnamed x8, local copies, waits for them, and re-layouts  5.78 us

profile of v3, /device:TPU:6, one launch (start us, length us, event | category | flops | bytes accessed | tf_op | source)
XLA Modules:
  0.0 153.3 jit_solution(7646460736783044018)
XLA Ops:
  0.6 0.0 copy-start
  0.7 0.8 copy.14
  1.5 0.1 reshape.45
  1.6 0.7 pad_add_fusion
  2.3 0.7 broadcast_in_dim.12.meta
  3.0 0.0 copy-done
  3.0 0.6 copy.17
  3.7 60.6 %front.1 = (bf16[256,512]{1,0:T(8,128)(2,1)}, s32[16,1024]{1,0:T(8,128)}, s32[8,128]{1,0:T(8,128)}, bf16[4,2,4,16,2048]{4,3,2,1,0:T(8,128)(2,1)}, bf16[4,2,4,16,512]{4,3,2,1,0:T(8,128)(2,1)}) custom-call(bf16[4,2,128,128]{3,2,1,0:T(8,128)(2,1)} %bitcast.27, bf16[4,16,2048]{2,1,0:T(8,128)(2,1)} %bitcast.28, bf16[4,16,512]{2,1,0:T(8,128)(2,1)} %bitcast.31, ...), custom_call_target="tpu_custom_call" | custom-call | tf_op jit(solution)/shard_map/front/pallas_call | solution.py:262
  64.3 12.9 %layer.1 = (bf16[256,512]{1,0:T(8,128)(2,1)}, bf16[256,512]{1,0:T(8,128)(2,1)}, bf16[512,2560]{1,0:T(8,128)(2,1)}) custom-call(s32[8,128]{1,0:T(8,128)} %get-tuple-element.15.lengths, bf16[256,512]{1,0:T(8,128)(2,1)} %get-tuple-element.16.rows, bf16[256,512]{1,0:T(8,128)(2,1)} %bitcast.25, bf16[512,2048]{1,0:T(8,128)(2,1)} %bitcast.23, bf16[512,512]{1,0:T(8,128)(2,1)} %bitcast.24), custom_call_target="tpu_custom_call" | custom-call | tf_op jit(solution)/shard_map/layer/pallas_call | solution.py:639
  77.2 71.2 %back.1 = (f32[128,128]{1,0:T(8,128)}, f32[64,2048]{1,0:T(8,128)}, f32[64,512]{1,0:T(8,128)}) custom-call(bf16[256,512]{1,0:T(8,128)(2,1)} %get-tuple-element.20.grads, s32[16,1024]{1,0:T(8,128)} %get-tuple-element.21.rows, bf16[4,2,4,16,2560]{4,3,2,1,0:T(8,128)(2,1)} %bitcast.22), custom_call_target="tpu_custom_call" | custom-call | tf_op jit(solution)/shard_map/back/pallas_call | solution.py:518
  148.4 1.5 copy.21
  149.9 1.9 %copy.22 = f32[64,2048]{1,0:T(8,128)} copy(f32[64,2048]{1,0:T(8,128)} %get-tuple-element.32) | data formatting | bytes 1048576
  151.8 1.6 %copy.23 = f32[64,512]{1,0:T(8,128)} copy(f32[64,512]{1,0:T(8,128)} %get-tuple-element.33) | data formatting | bytes 262144
  (2 shorter events, 0.0 us)
Async XLA Ops:
  0.6 2.4 %copy-start = (s32[1,16384,16]{1,2,0:T(8,128)S(1)}, s32[1,16384,16]{1,2,0:T(8,128)}, u32[]{:S(2)}) copy-start(s32[1,16384,16]{1,2,0:T(8,128)} %param.8) | copy-start | bytes 3145732

commit v4 on v3

v4 whole, which is shorter than its diff:
```python
import functools

import jax
import jax.numpy as jnp
from jax import lax
from jax.experimental import pallas as pl
from jax.experimental.pallas import tpu as pltpu
from jax.sharding import PartitionSpec as P

D = 512
HEADS = 8
COLS = 128
DISTINCT = 1024
SLOT = 128
NSEQ = 2
TABLES = 16
NZ = 16
NX = 4
NY = 4
NB = 8
EPS = 1e-05
BF = jnp.bfloat16
F32 = jnp.float32
VMEM_LIMIT = 64000 * 1024


def place():
    emb = lax.axis_index("emb")
    bal = lax.axis_index("bal")
    return emb // NX, emb % NX, bal // 2, bal % 2


def at(z, x, y, k):
    return {"emb": z * NX + x, "bal": y * 2 + k}


def rcopy(src, dst, send, recv, device):
    return pltpu.make_async_remote_copy(
        src_ref=src,
        dst_ref=dst,
        send_sem=send,
        recv_sem=recv,
        device_id=device,
        device_id_type=pl.DeviceIdType.MESH,
    )


def greet(devices):
    barrier = pltpu.get_barrier_semaphore()
    for device in devices:
        pl.semaphore_signal(barrier, inc=1, device_id=device, device_id_type=pl.DeviceIdType.MESH)
    pl.semaphore_wait(barrier, len(devices))


VM = pl.BlockSpec(memory_space=pltpu.VMEM)
ANY = pl.BlockSpec(memory_space=pl.ANY)
DMA = pltpu.SemaphoreType.DMA


ARRIVALS = (1, -1, 4, -4, 2, -2, 3, -3, 5, -5, 6, -6, 7, -7, 8)
INDEX = {offset: i for i, offset in enumerate(ARRIVALS)}
FIRST = (4, -4, 1, -1, 2, -2, 3, -3)
RELAYS = {4: (1, 2, 3, 4), -4: (-1, -2, -3)}


def front_kernel(
    tab, win, wout, ids, lengths, surpluses, helpers, out, id_rows, lens, wfi, wfo,
    tabs, idall, metall, columns, total, looked, meta,
    zs, zr, ys, yr, cs, cr, ws, wr, os_, or_, is_, ir, ms, mr, es, er, loc,
):
    z, x, y, k = place()
    bal = y * 2 + k
    y_peers = [(y + 1) % NY, (y + 3) % NY, (y + 2) % NY]
    x_peers = [(x + 1) % NX, (x + 3) % NX, (x + 2) % NX]
    y_from = [y_peers[1], y_peers[0], y_peers[2]]
    x_from = [x_peers[1], x_peers[0], x_peers[2]]
    y_devices = [at(z, x, peer, k) for peer in y_peers]
    x_devices = [at(z, peer, y, k) for peer in x_peers]
    other = at(z, x, y, 1 - k)
    z_devices = {o: at((z + o + NZ) % NZ, x, y, k) for o in FIRST}
    greet(list(z_devices.values()) + y_devices + x_devices + [other])

    sent = []

    def go(src, dst, send, recv, device):
        copy = rcopy(src, dst, send, recv, device)
        copy.start()
        sent.append(copy)

    def came(dst, send, recv):
        rcopy(dst, dst, send, recv, other).wait_recv()

    def origin(offset):
        return (z + NZ - offset) % NZ

    meta[0:8, :] = jnp.broadcast_to(lengths[:, 0:1], (NB, 128))
    meta[8:16, :] = jnp.broadcast_to(lengths[:, 1:2], (NB, 128))
    meta[16:24, :] = jnp.broadcast_to(surpluses[...], (NB, 128))
    meta[24:32, :] = jnp.broadcast_to(helpers[...], (NB, 128))
    for o in FIRST:
        i = INDEX[o]
        go(tab.at[y, k], tabs.at[z, y, k], zs.at[i], zr.at[i], z_devices[o])
    for i in range(3):
        go(ids, idall.at[y, k], is_.at[i], ir.at[i], y_devices[i])
        go(meta, metall.at[x], ms.at[i], mr.at[i], x_devices[i])
    for i in range(3):
        go(win.at[x], wfi.at[y, k, x], ws.at[i], wr.at[i], y_devices[i])
        go(wout.at[x], wfo.at[y, k, x], os_.at[i], or_.at[i], y_devices[i])
    local = [
        pltpu.make_async_copy(win.at[x], wfi.at[y, k, x], loc.at[0]),
        pltpu.make_async_copy(wout.at[x], wfo.at[y, k, x], loc.at[1]),
        pltpu.make_async_copy(ids, idall.at[y, k], loc.at[2]),
        pltpu.make_async_copy(meta, metall.at[x], loc.at[3]),
    ]
    for copy in local:
        copy.start()

    def from_z(pair):
        i, zz = INDEX[pair], origin(pair)
        mine = tabs.at[zz, y, k]
        came(mine, zs.at[i], zr.at[i])
        for r in RELAYS.get(pair, ()):
            j = INDEX[pair + r]
            go(mine, mine, zs.at[j], zr.at[j], z_devices[r])
        for p in range(3):
            go(mine, mine, ys.at[i, p], yr.at[i, p], y_devices[p])

    def from_y(pair):
        i, zz = INDEX[pair], origin(pair)
        for p in range(3):
            came(tabs.at[zz, y_from[p], k], ys.at[i, p], yr.at[i, p])
        go(tabs.at[zz, :, k], tabs.at[zz, :, k], cs.at[i], cr.at[i], other)

    def from_core(pair):
        i, zz = INDEX[pair], origin(pair)
        came(tabs.at[zz, :, 1 - k], cs.at[i], cr.at[i])

    lane = lax.broadcasted_iota(jnp.int32, (8 * SLOT, TABLES), 1)
    vocab = lax.broadcasted_iota(jnp.int32, (8 * SLOT, 256), 1)

    def sum_table(t, read):
        picked = jnp.sum(jnp.where(lane == t, columns[...], 0), axis=1, keepdims=True)

        def body(part, carry):
            hot = jnp.where(picked - part * 256 == vocab, 1.0, 0.0).astype(BF)
            total[...] += jnp.dot(hot, read(part), preferred_element_type=F32)
            return carry

        lax.fori_loop(0, 4, body, 0)

    def read_own(part):
        return tab[part].reshape(256, COLS)

    def choose_ids():
        for i in range(3):
            came(metall.at[x_from[i]], ms.at[i], mr.at[i])
        local[3].wait()
        came(idall.at[:, 1 - k], is_.at[3], ir.at[3])
        for xx in range(NX):
            mine = jnp.zeros((1, SLOT), jnp.int32)
            moved = jnp.zeros((TABLES, SLOT), jnp.int32)
            for b in range(NB):
                surplus = metall[xx, 16 + b:17 + b, :]
                is_mine = jnp.where(bal == b, 1, 0)
                mine = mine + surplus * is_mine
                sends = jnp.where(metall[xx, 24 + b:25 + b, :] == bal, 1, 0)
                first = idall[b // 2, b % 2, 2 * xx]
                second = idall[b // 2, b % 2, 2 * xx + 1]
                moved = moved + sends * (first + surplus * (second - first))
            for s in range(NSEQ):
                away = mine if s == 1 else 1 - mine
                kept = idall[y, k, 2 * xx + s]
                chosen = kept + away * (moved - kept)
                i = 2 * xx + s
                id_rows[:, i * SLOT:(i + 1) * SLOT] = chosen
                columns[i * SLOT:(i + 1) * SLOT, :] = jnp.transpose(chosen)
        mine = jnp.zeros((1, SLOT), jnp.int32)
        moved = jnp.zeros((1, SLOT), jnp.int32)
        kept = [jnp.zeros((1, SLOT), jnp.int32) for _ in range(NSEQ)]
        for b in range(NB):
            surplus = metall[x, 16 + b:17 + b, :]
            is_mine = jnp.where(bal == b, 1, 0)
            mine = mine + surplus * is_mine
            sends = jnp.where(metall[x, 24 + b:25 + b, :] == bal, 1, 0)
            first = metall[x, b:b + 1, :]
            second = metall[x, 8 + b:9 + b, :]
            moved = moved + sends * (first + surplus * (second - first))
            kept[0] = kept[0] + is_mine * first
            kept[1] = kept[1] + is_mine * second
        lens[...] = jnp.zeros_like(lens)
        lens[0:1, :] = kept[0] + (1 - mine) * (moved - kept[0])
        lens[1:2, :] = kept[1] + mine * (moved - kept[1])

    def ids_core():
        local[2].wait()
        for i in range(3):
            came(idall.at[y_from[i], k], is_.at[i], ir.at[i])
        go(idall.at[:, k], idall.at[:, k], is_.at[3], ir.at[3], other)

    def weights_x():
        local[0].wait()
        local[1].wait()
        for full, s_, r_ in ((wfi, ws, wr), (wfo, os_, or_)):
            for i in range(3):
                came(full.at[y_from[i], k, x], s_.at[i], r_.at[i])
            for i in range(3):
                part = full.at[:, k, x]
                go(part, part, s_.at[3 + i], r_.at[3 + i], x_devices[i])

    def weights_core():
        for full, s_, r_ in ((wfi, ws, wr), (wfo, os_, or_)):
            for i in range(3):
                came(full.at[:, k, x_from[i]], s_.at[3 + i], r_.at[3 + i])
            go(full.at[:, k], full.at[:, k], s_.at[6], r_.at[6], other)

    total[...] = jnp.zeros_like(total)
    for pair in ARRIVALS[:4]:
        from_z(pair)
    ids_core()
    for pair in ARRIVALS[4:8]:
        from_z(pair)
    from_y(ARRIVALS[0])
    choose_ids()
    sum_table(z, read_own)
    weights_x()
    for n in range(15):
        if n < 7:
            from_z(ARRIVALS[8 + n])
        if n < 14:
            from_y(ARRIVALS[n + 1])
        if n == 13:
            weights_core()
        from_core(ARRIVALS[n])
        zz = origin(ARRIVALS[n])
        sum_table(zz, lambda part, zz=zz: tabs[zz, part].reshape(256, COLS))

    looked[...] = total[...].astype(BF).reshape(NX, 256, COLS)

    def piece(i):
        return out.at[:, pl.ds(pl.multiple_of(i * COLS, COLS), COLS)]

    for i in (2, 0, 1):
        go(looked.at[x_peers[i]], piece(x), es.at[i], er.at[i], x_devices[i])
    own = pltpu.make_async_copy(looked.at[x], piece(x), loc.at[4])
    own.start()
    came(wfi.at[:, 1 - k], ws.at[6], wr.at[6])
    came(wfo.at[:, 1 - k], os_.at[6], or_.at[6])
    for i in range(3):
        came(piece(x_from[i]), es.at[i], er.at[i])
    own.wait()
    for copy in sent:
        copy.wait_send()


def front(tab, win, wout, ids, lengths, surpluses, helpers):
    v = pltpu.VMEM
    return pl.pallas_call(
        front_kernel,
        name="front",
        out_shape=(
            jax.ShapeDtypeStruct((256, D), BF),
            jax.ShapeDtypeStruct((TABLES, 8 * SLOT), jnp.int32),
            jax.ShapeDtypeStruct((8, SLOT), jnp.int32),
            jax.ShapeDtypeStruct((NY, 2, NX, 16, 2048), BF),
            jax.ShapeDtypeStruct((NY, 2, NX, 16, 512), BF),
        ),
        in_specs=[VM] * 7,
        out_specs=(VM, VM, VM, ANY, ANY),
        scratch_shapes=[
            v((NZ, NY, 2, 128, COLS), BF),
            v((NY, 2, 8, TABLES, SLOT), jnp.int32),
            v((NX, 32, 128), jnp.int32),
            v((8 * SLOT, TABLES), jnp.int32),
            v((8 * SLOT, COLS), F32),
            v((NX, 256, COLS), BF),
            v((32, 128), jnp.int32),
            DMA((15,)), DMA((15,)), DMA((15, 3)), DMA((15, 3)), DMA((15,)), DMA((15,)),
            DMA((7,)), DMA((7,)), DMA((7,)), DMA((7,)), DMA((4,)), DMA((4,)),
            DMA((3,)), DMA((3,)), DMA((3,)), DMA((3,)), DMA((5,)),
        ],
        compiler_params=pltpu.CompilerParams(
            collective_id=0, has_side_effects=True, vmem_limit_bytes=VMEM_LIMIT
        ),
    )(tab, win, wout, ids, lengths, surpluses, helpers)


def silu_grad(argument):
    logistic = jax.nn.sigmoid(argument)
    return logistic * (1.0 + argument * (1.0 - logistic))


def normalize(values):
    average = jnp.mean(values, axis=1, keepdims=True)
    centred = values - average
    inverse = lax.rsqrt(jnp.mean(centred * centred, axis=1, keepdims=True) + EPS)
    return centred * inverse, inverse


def norm_back(incoming, normed, inverse):
    first = jnp.mean(incoming, axis=1, keepdims=True)
    second = jnp.mean(incoming * normed, axis=1, keepdims=True)
    return inverse * (incoming - first - normed * second)


def dot(a, b, ca, cb):
    return lax.dot_general(a, b, (((ca,), (cb,)), ((), ())), preferred_element_type=F32)


def run_layer(lengths, rows, cot, w_in, w_out, out, grad, wg, act, proj, att, gh, wg_done):
    width = D // HEADS
    scale = width ** (-0.5)
    values = rows[...].astype(F32)
    normed_in, in_inverse = normalize(values)
    half_in = normed_in.astype(BF)
    projected = dot(half_in, w_in[...], 1, 0)
    proj[...] = projected
    activated = jax.nn.silu(projected)
    gate = activated[:, :D]
    act[...] = activated[:, D:].astype(BF)
    place_i = lax.broadcasted_iota(jnp.int32, (SLOT, SLOT), 0)
    place_j = lax.broadcasted_iota(jnp.int32, (SLOT, SLOT), 1)
    masks = [
        (place_j <= place_i) & (place_i < lengths[s:s + 1, :]) for s in range(NSEQ)
    ]

    def heads(s, h):
        r = slice(s * SLOT, (s + 1) * SLOT)
        v = act[r, h * width:(h + 1) * width]
        q = act[r, D + h * width:D + (h + 1) * width]
        key = act[r, 2 * D + h * width:2 * D + (h + 1) * width]
        return r, v, q, key

    for s in range(NSEQ):
        for h in range(HEADS):
            r, v, q, key = heads(s, h)
            scores = dot(q, key, 1, 1) * scale
            weights = jnp.where(masks[s], jax.nn.silu(scores) * (1.0 / SLOT), 0.0).astype(BF)
            att[r, h * width:(h + 1) * width] = dot(weights, v, 1, 0)
    normed_out, out_inverse = normalize(att[...])
    mixed = (normed_out * gate).astype(BF)
    out[...] = (values + dot(mixed, w_out[...], 1, 0)).astype(BF)
    cotangent = cot[...]
    wg[:, :, :, :, 4 * D:] = (
        dot(mixed, cotangent, 0, 0).astype(BF).reshape(NY, 2, NX, 16, D)
    )
    grad_mixed = dot(cotangent, w_out[...], 1, 1)
    att[...] = norm_back(grad_mixed * gate, normed_out, out_inverse)
    gh[:, :D] = (grad_mixed * normed_out * silu_grad(proj[:, :D])).astype(BF)
    for s in range(NSEQ):
        for h in range(HEADS):
            r, v, q, key = heads(s, h)
            g = att[r, h * width:(h + 1) * width].astype(BF)
            scores = dot(q, key, 1, 1) * scale
            logistic = jax.nn.sigmoid(scores)
            weights = jnp.where(masks[s], scores * logistic * (1.0 / SLOT), 0.0).astype(BF)
            slope = logistic * (1.0 + scores * (1.0 - logistic))
            gw = dot(g, v, 1, 1)
            gs = jnp.where(masks[s], gw * (1.0 / SLOT) * slope, 0.0).astype(BF)
            parts = (
                dot(weights, g, 0, 0), dot(gs, key, 1, 0) * scale, dot(gs, q, 0, 0) * scale
            )
            for p in range(3):
                c = slice(D + p * D + h * width, D + p * D + (h + 1) * width)
                gh[r, c] = (parts[p] * silu_grad(proj[r, c])).astype(BF)
    grad_projected = gh[...]
    wg[:, :, :, :, :4 * D] = (
        dot(half_in, grad_projected, 0, 0).astype(BF).reshape(NY, 2, NX, 16, 4 * D)
    )
    wg_done()
    grad_normed = dot(grad_projected, w_in[...], 1, 1)
    grad[...] = (
        cotangent.astype(F32) + norm_back(grad_normed, normed_in, in_inverse)
    ).astype(BF)


OFFSETS = (2, 1, -1, 0)
FAR_FIRST = (8, 7, 9, 6, 10, 5, 11, 4, 12, 3, 13, 2, 14, 1, 15)


def back_kernel(
    lengths, x_rows, cot, w_in, w_out, rows,
    layer_out, tout, we,
    grads, wg, act, proj, att, gh, gx, to, t1, ta, tl1, tr1, tl2, tr2, tb, tz1, ts, tz2,
    w1, wa, wp, wl1, wr1, wl, wr, wl2, wr2, wc, wz, wd,
    gs, gr, cs, cr, ys, yr, zs, zr, z2s, z2r, loc,
    wcs, wcr, wls, wlr, wrs, wrr, wzs, wzr, wgs, wgr, wes, wer,
):
    z, x, y, k = place()
    yp, ym, y2 = (y + 1) % NY, (y + 3) % NY, (y + 2) % NY
    xp, xm, x2 = (x + 1) % NX, (x + 3) % NX, (x + 2) % NX
    up, down = at(z, x, yp, k), at(z, x, ym, k)
    east, west, far = at(z, xp, y, k), at(z, xm, y, k), at(z, x2, y, k)
    other = at(z, x, y, 1 - k)
    x_peers, x_from, x_devices = (xp, xm, x2), (xm, xp, x2), (east, west, far)
    y_peers, y_devices = (yp, ym, y2), (up, down, at(z, x, y2, k))
    ring = {o: (z + o) % NZ for o in range(1, NZ)}
    greeted = [*y_devices, *x_devices, other] + [at(ring[o], x, y, k) for o in range(1, NZ)]
    barrier = pltpu.get_barrier_semaphore()
    for device in greeted:
        pl.semaphore_signal(barrier, inc=1, device_id=device, device_id_type=pl.DeviceIdType.MESH)

    sent = []

    def go(src, dst, send, recv, device):
        copy = rcopy(src, dst, send, recv, device)
        copy.start()
        sent.append(copy)

    def came(dst, send, recv):
        rcopy(dst, dst, send, recv, other).wait_recv()

    def add(*values):
        total = values[0].astype(F32)
        for value in values[1:]:
            total = total + value.astype(F32)
        return total

    chosen_sent = []

    def choose(condition, src, dst, send, recv, zz):
        both = rcopy(src, dst, send, recv, at(zz, x, y, k))
        one = rcopy(src.at[0], dst.at[0], send, recv, at(zz, x, y, k))

        @pl.when(condition)
        def _():
            both.start()

        @pl.when(jnp.logical_not(condition))
        def _():
            one.start()

        chosen_sent.append((condition, both, one))

    def chosen(condition, dst, send, recv):
        @pl.when(condition)
        def _():
            came(dst, send, recv)

        @pl.when(jnp.logical_not(condition))
        def _():
            came(dst.at[0], send, recv)

    def columns(i):
        return grads.at[:, pl.ds(pl.multiple_of(i * COLS, COLS), COLS)]

    def weights_ready():
        pl.semaphore_wait(barrier, len(greeted))
        go(wg.at[:, 1 - k], w1, wcs, wcr, other)

    run_layer(
        lengths, x_rows, cot, w_in, w_out, layer_out, grads, wg, act, proj, att, gh, weights_ready
    )

    for i, (peer, device) in enumerate(((x2, far), (xp, east), (xm, west))):
        go(columns(peer), gx.at[x], gs.at[i], gr.at[i], device)
    own = pltpu.make_async_copy(columns(x), gx.at[x], loc.at[0])
    own.start()

    place_row = lax.broadcasted_iota(jnp.int32, (128, 8 * SLOT), 0)

    def rows_of(q, core, out):
        residue = (z + OFFSETS[q] + NZ) % 4

        def body(i, carry):
            picked = rows[pl.ds(i * 4 + residue, 1), :] - core * 128
            hot = jnp.concatenate(
                [
                    jnp.where(picked - part * 256 == place_row, 1.0, 0.0).astype(BF)
                    for part in range(4)
                ],
                axis=0,
            )
            found = jnp.dot(
                hot, gx[...].reshape(8 * SLOT, COLS), preferred_element_type=F32
            ).astype(BF)
            out[q, i] = found.reshape(NY, 128, COLS)
            return carry

        lax.fori_loop(0, 4, body, 0)

    def compute(q):
        rows_of(q, 1 - k, to)
        go(to.at[q], t1.at[q], cs.at[q], cr.at[q], other)
        rows_of(q, k, ta)

    def t_core(q):
        came(t1.at[q], cs.at[q], cr.at[q])
        for i in range(4):
            ta[q, i] = add(ta[q, i], t1[q, i]).astype(BF)
        go(ta.at[q, :, y2, 0:64], tl1.at[q], ys.at[q, 0], yr.at[q, 0], up)
        go(ta.at[q, :, y2, 64:128], tr1.at[q], ys.at[q, 1], yr.at[q, 1], down)

    def t_y(q):
        came(tl1.at[q], ys.at[q, 0], yr.at[q, 0])
        ta[q, :, yp, 0:64] = add(ta[q, :, yp, 0:64], tl1[q]).astype(BF)
        go(ta.at[q, :, yp], tl2.at[q], ys.at[q, 2], yr.at[q, 2], up)
        came(tr1.at[q], ys.at[q, 1], yr.at[q, 1])
        ta[q, :, ym, 64:128] = add(ta[q, :, ym, 64:128], tr1[q]).astype(BF)
        go(ta.at[q, :, ym], tr2.at[q], ys.at[q, 3], yr.at[q, 3], down)

    def t_z(q):
        came(tl2.at[q], ys.at[q, 2], yr.at[q, 2])
        came(tr2.at[q], ys.at[q, 3], yr.at[q, 3])
        tb[q] = add(ta[q, :, y], tl2[q], tr2[q]).astype(BF)
        if q < 3:
            device = at((z + OFFSETS[q] + NZ) % NZ, x, y, k)
            go(tb.at[q], tz1.at[q], zs.at[q], zr.at[q], device)

    def t_z2():
        for q in range(3):
            came(tz1.at[q], zs.at[q], zr.at[q])
        ts[...] = add(tb[3], tz1[0], tz1[1], tz1[2]).astype(BF)
        for m in (2, 1, 3):
            zz = (z + 4 * m) % NZ
            go(ts.at[zz // 4], tz2.at[m - 1], z2s.at[m - 1], z2r.at[m - 1], at(zz, x, y, k))

    def t_end():
        total = ts[z // 4].astype(F32)
        for m in range(3):
            came(tz2.at[m], z2s.at[m], z2r.at[m])
            total = total + tz2[m].astype(F32)
        tout[...] = total

    def w_core():
        came(w1, wcs, wcr)
        for i in range(4):
            wa[i] = add(wg[i, k], w1[i]).astype(BF)
        for i in range(3):
            for j in range(NY):
                wp[i, j] = wa[j, x_peers[i], :, 0:1280]
        for i in range(3):
            go(wp.at[i], wl1.at[i], wls.at[0, i], wlr.at[0, i], x_devices[i])
            part = wa.at[y_peers[i], :, :, 1280:2560]
            go(part, wr1.at[i], wrs.at[0, i], wrr.at[0, i], y_devices[i])

    def w_first():
        for i in range(3):
            came(wl1.at[i], wls.at[0, i], wlr.at[0, i])
        wl[...] = add(wa[:, x, :, 0:1280], wl1[0], wl1[1], wl1[2]).astype(BF)
        for i in range(3):
            go(wl.at[y_peers[i]], wl2.at[i], wls.at[1, i], wlr.at[1, i], y_devices[i])
        for i in range(3):
            came(wr1.at[i], wrs.at[0, i], wrr.at[0, i])
        wr[...] = add(wa[y, :, :, 1280:2560], wr1[0], wr1[1], wr1[2]).astype(BF)
        for i in range(3):
            go(wr.at[x_peers[i]], wr2.at[i], wrs.at[1, i], wrr.at[1, i], x_devices[i])

    def w_second():
        for i in range(3):
            came(wl2.at[i], wls.at[1, i], wlr.at[1, i])
            came(wr2.at[i], wrs.at[1, i], wrr.at[1, i])
        low = add(wl[y], wl2[0], wl2[1], wl2[2]).astype(BF)
        high = add(wr[x], wr2[0], wr2[1], wr2[2]).astype(BF)
        tiles = [low[:, j * 128:(j + 1) * 128] for j in range(10)]
        tiles += [high[:, j * 128:(j + 1) * 128] for j in range(10)]
        for j in range(NZ):
            wc[j, 0] = tiles[j]
            wc[j, 1] = tiles[16 + j // 4]
        for o in FAR_FIRST:
            zz = ring[o]
            choose(zz % 4 == 0, wc.at[zz], wz.at[o - 1], wzs.at[o - 1], wzr.at[o - 1], zz)

    def w_z():
        for o in range(1, NZ):
            chosen(z % 4 == 0, wz.at[o - 1], wzs.at[o - 1], wzr.at[o - 1])
        total = wc[z].astype(F32)
        for o in range(1, NZ):
            total = total + wz[o - 1].astype(F32)
        wd[z] = total.astype(BF)
        for o in FAR_FIRST:
            choose(z % 4 == 0, wd.at[z], wd.at[z], wgs.at[o - 1], wgr.at[o - 1], ring[o])

    def w_z2():
        for o in range(1, NZ):
            zz = (z + NZ - o) % NZ
            chosen(zz % 4 == 0, wd.at[zz], wgs.at[o - 1], wgr.at[o - 1])
        for j in range(16):
            we[x, :, j * 128:(j + 1) * 128] = wd[j, 0]
        for c in range(4):
            we[x, :, 2048 + c * 128:2048 + (c + 1) * 128] = wd[4 * c, 1]
        for i in range(3):
            go(we.at[x], we.at[x], wes.at[i], wer.at[i], x_devices[i])

    def w_end():
        for i in range(3):
            came(we.at[x_from[i]], wes.at[i], wer.at[i])

    w_core()
    own.wait()
    for i, source in enumerate((x2, xm, xp)):
        came(gx.at[source], gs.at[i], gr.at[i])
    compute(0)
    t_core(0)
    compute(1)
    t_core(1)
    t_y(0)
    w_first()
    compute(2)
    t_core(2)
    t_y(1)
    t_z(0)
    w_second()
    compute(3)
    t_core(3)
    t_y(2)
    t_z(1)
    t_y(3)
    t_z(2)
    w_z()
    t_z(3)
    t_z2()
    w_z2()
    t_end()
    w_end()
    for copy in sent:
        copy.wait_send()
    for condition, both, one in chosen_sent:

        @pl.when(condition)
        def _():
            both.wait_send()

        @pl.when(jnp.logical_not(condition))
        def _():
            one.wait_send()


def back(lengths, x_rows, cot, w_in, w_out, rows):
    v = pltpu.VMEM
    return pl.pallas_call(
        back_kernel,
        name="back",
        out_shape=(
            jax.ShapeDtypeStruct((256, D), BF),
            jax.ShapeDtypeStruct((128, COLS), F32),
            jax.ShapeDtypeStruct((NX, 16, 2560), BF),
        ),
        in_specs=[VM] * 6,
        out_specs=(VM,) * 3,
        scratch_shapes=[
            v((256, D), BF), v((NY, 2, NX, 16, 2560), BF),
            v((256, 3 * D), BF), v((256, 4 * D), F32), v((256, D), F32), v((256, 4 * D), BF),
            v((NX, 256, COLS), BF), v((4, 4, NY, 128, COLS), BF),
            v((4, 4, NY, 128, COLS), BF), v((4, 4, NY, 128, COLS), BF),
            v((4, 4, 64, COLS), BF), v((4, 4, 64, COLS), BF),
            v((4, 4, 128, COLS), BF), v((4, 4, 128, COLS), BF),
            v((4, 4, 128, COLS), BF), v((3, 4, 128, COLS), BF),
            v((4, 128, COLS), BF), v((3, 128, COLS), BF),
            v((NY, NX, 16, 2560), BF), v((NY, NX, 16, 2560), BF),
            v((3, NY, 16, 1280), BF), v((3, NY, 16, 1280), BF), v((3, NX, 16, 1280), BF),
            v((NY, 16, 1280), BF), v((NX, 16, 1280), BF),
            v((3, 16, 1280), BF), v((3, 16, 1280), BF),
            v((NZ, 2, 16, 128), BF), v((15, 2, 16, 128), BF),
            v((NZ, 2, 16, 128), BF),
            DMA((3,)), DMA((3,)),
            DMA((4,)), DMA((4,)), DMA((4, 4)), DMA((4, 4)), DMA((3,)), DMA((3,)),
            DMA((3,)), DMA((3,)), DMA((2,)),
            DMA, DMA, DMA((2, 3)), DMA((2, 3)), DMA((2, 3)), DMA((2, 3)),
            DMA((15,)), DMA((15,)), DMA((15,)), DMA((15,)), DMA((3,)), DMA((3,)),
        ],
        compiler_params=pltpu.CompilerParams(
            collective_id=3, has_side_effects=True, vmem_limit_bytes=VMEM_LIMIT
        ),
    )(lengths, x_rows, cot, w_in, w_out, rows)


def finish_kernel(table_scale, grad_scale, layer_in, table_in, we, layer_out, table, gin, gout):
    layer_out[...] = layer_in[...]
    table[...] = table_in[...] * table_scale
    for i in range(NX):
        total = we[i].astype(F32) * grad_scale
        gin[i * 16:(i + 1) * 16, :] = total[:, :2048]
        gout[i * 16:(i + 1) * 16, :] = total[:, 2048:]


def finish(layer_out, table_sum, weight_sum, table_scale, grad_scale):
    return pl.pallas_call(
        functools.partial(finish_kernel, table_scale, grad_scale),
        name="finish",
        out_shape=(
            jax.ShapeDtypeStruct((256, D), BF),
            jax.ShapeDtypeStruct((128, COLS), F32),
            jax.ShapeDtypeStruct((64, 2048), F32),
            jax.ShapeDtypeStruct((64, 512), F32),
        ),
        in_specs=[VM] * 3,
        out_specs=(VM,) * 4,
    )(layer_out, table_sum, weight_sum)


def on_device(
    item_ids, seq_lengths, surplus_slot, helper_map, embed_tables, weight_in, weight_out, cotangent
):
    z = lax.axis_index("emb") // NX
    near = lax.dynamic_slice_in_dim(item_ids[0], z * 1024, 1024, 0)
    ids = jnp.transpose(near.reshape(8, SLOT, TABLES), (0, 2, 1))
    rows, id_rows, lengths, w_in, w_out = front(
        embed_tables.reshape(NY, 2, 128, COLS),
        weight_in.reshape(NX, 16, 2048),
        weight_out.reshape(NX, 16, 512),
        ids,
        seq_lengths.reshape(NB, NSEQ),
        surplus_slot,
        helper_map,
    )
    layer_out, table_sum, weight_sum = back(
        lengths, rows, cotangent[0], w_in.reshape(D, 4 * D), w_out.reshape(D, D), id_rows
    )
    events = NB * item_ids.shape[1]
    layer_out, table_grad, grad_in, grad_out = finish(
        layer_out, table_sum, weight_sum, (DISTINCT / events) ** 0.5, events ** (-0.5)
    )
    return layer_out[None], table_grad[None], grad_in, grad_out


def solution(mesh):
    placed = (
        P("bal", None, None),
        P(None, "emb", None),
        P(None, "emb"),
        P(None, "emb"),
        P("emb", None, None),
        P("bal", None),
        P("bal", None),
        P("bal", "emb", None),
    )
    return jax.shard_map(
        on_device,
        mesh=mesh,
        in_specs=placed,
        out_specs=(P("bal", "emb", None), P("emb", "bal", None), P("bal", None), P("bal", None)),
        check_vma=False,
    )
```

time: 154 us -> 134 us (0.87)
  Pallas kernels: 145 us -> 127 us
  local copies, waits for them, and re-layouts: 7.18 us -> 4.74 us
    pallas_call x2, Pallas kernels: 84.1 us -> 67.6 us  [the longest x1 65.6 us: back(): pl.pallas_call(back_kernel, name='back', out_shape=(jax.ShapeDtypeStruct(...]
    unnamed x8 -> x6, local copies, waits for them, and re-layouts: 5.78 us -> 2.67 us
    pallas_call x1, Pallas kernels: 60.6 us -> 58.9 us  [front(): pl.pallas_call(front_kernel, name='front', out_shape=(jax.ShapeDtypeStruc...]
where the time goes in v4:
time: 134 us; the launch traced here: 132 us
  Pallas kernels  127 us (95%)
  local copies, waits for them, and re-layouts  4.74 us (4%)
    pallas_call x1, Pallas kernels, back(): pl.pallas_call(back_kernel, name='back', out_shape=(jax.ShapeDtypeStruct(...  65.6 us
    pallas_call x1, Pallas kernels, front(): pl.pallas_call(front_kernel, name='front', out_shape=(jax.ShapeDtypeStruc...  58.9 us

profile of v4, /device:TPU:6, one launch (start us, length us, event | category | flops | bytes accessed | tf_op | source)
XLA Modules:
  0.0 131.9 jit_solution(13724514974264855810)
XLA Ops:
  0.6 0.0 copy-start
  0.7 1.4 %copy.16.lengths = s32[8,2]{1,0:T(8,128)} copy(s32[8,2]{0,1:T(2,128)} %bitcast.26) | data formatting | bytes 128 | tf_op jit(solution)/shard_map/reshape | solution.py:702
  2.1 1.3 %copy.17.surpluses = s32[8,1]{1,0:T(8,128)} copy(s32[8,1]{0,1:T(1,128)} %param.10) | data formatting | bytes 64 | tf_op args[2]
  3.4 1.3 %copy.18.helpers = s32[8,1]{1,0:T(8,128)} copy(s32[8,1]{0,1:T(1,128)} %param.11) | data formatting | bytes 64 | tf_op args[3]
  4.7 0.0 copy-done
  4.8 0.6 copy.21
  5.4 58.9 %front.1 = (bf16[256,512]{1,0:T(8,128)(2,1)}, s32[16,1024]{1,0:T(8,128)}, s32[8,128]{1,0:T(8,128)}, bf16[4,2,4,16,2048]{4,3,2,1,0:T(8,128)(2,1)}, bf16[4,2,4,16,512]{4,3,2,1,0:T(8,128)(2,1)}) custom-call(bf16[4,2,128,128]{3,2,1,0:T(8,128)(2,1)} %bitcast.22, bf16[4,16,2048]{2,1,0:T(8,128)(2,1)} %bitcast.23, bf16[4,16,512]{2,1,0:T(8,128)(2,1)} %bitcast.25, ...), custom_call_target="tpu_custom_call" | custom-call | tf_op jit(solution)/shard_map/front/pallas_call | solution.py:257
  64.3 65.6 %back.1 = (bf16[256,512]{1,0:T(8,128)(2,1)}, f32[128,128]{1,0:T(8,128)}, bf16[4,16,2560]{2,1,0:T(8,128)(2,1)}) custom-call(s32[8,128]{1,0:T(8,128)} %get-tuple-element.16.lengths, bf16[256,512]{1,0:T(8,128)(2,1)} %get-tuple-element.17.x_rows, bf16[256,512]{1,0:T(8,128)(2,1)} %bitcast.20, bf16[512,2048]{1,0:T(8,128)(2,1)} %bitcast.18, ...), custom_call_target="tpu_custom_call" | custom-call | tf_op jit(solution)/shard_map/back/pallas_call | solution.py:630
  129.9 2.0 %finish.1 = (bf16[256,512]{1,0:T(8,128)(2,1)}, f32[128,128]{1,0:T(8,128)}, f32[64,2048]{1,0:T(8,128)}, f32[64,512]{1,0:T(8,128)}) custom-call(bf16[256,512]{1,0:T(8,128)(2,1)} %get-tuple-element.21.layer_in, f32[128,128]{1,0:T(8,128)} %get-tuple-element.22.table_in, bf16[4,16,2560]{2,1,0:T(8,128)(2,1)} %get-tuple-element.23.we), custom_call_target="tpu_custom_call" | custom-call | tf_op jit(solution)/shard_map/finish/pallas_call | solution.py:677
  (2 shorter events, 0.0 us)
Async XLA Ops:
  0.6 4.1 %copy-start = (s32[1,16384,16]{1,2,0:T(8,128)S(1)}, s32[1,16384,16]{1,2,0:T(8,128)}, u32[]{:S(2)}) copy-start(s32[1,16384,16]{1,2,0:T(8,128)} %param.8) | copy-start | bytes 3145732

commit v5 on v4

--- a/solution.py
+++ b/solution.py
@@ -64,7 +64,7 @@
 
 
 def front_kernel(
-    tab, win, wout, ids, lengths, surpluses, helpers, out, id_rows, lens, wfi, wfo,
+    tab, win, wout, ids, facts, out, id_rows, lens, wfi, wfo,
     tabs, idall, metall, columns, total, looked, meta,
     zs, zr, ys, yr, cs, cr, ws, wr, os_, or_, is_, ir, ms, mr, es, er, loc,
 ):
@@ -93,10 +93,8 @@
     def origin(offset):
         return (z + NZ - offset) % NZ
 
-    meta[0:8, :] = jnp.broadcast_to(lengths[:, 0:1], (NB, 128))
-    meta[8:16, :] = jnp.broadcast_to(lengths[:, 1:2], (NB, 128))
-    meta[16:24, :] = jnp.broadcast_to(surpluses[...], (NB, 128))
-    meta[24:32, :] = jnp.broadcast_to(helpers[...], (NB, 128))
+    for i in range(4):
+        meta[8 * i:8 * i + 8, :] = jnp.broadcast_to(facts[:, i:i + 1], (NB, 128))
     for o in FIRST:
         i = INDEX[o]
         go(tab.at[y, k], tabs.at[z, y, k], zs.at[i], zr.at[i], z_devices[o])
@@ -252,7 +250,7 @@
         copy.wait_send()
 
 
-def front(tab, win, wout, ids, lengths, surpluses, helpers):
+def front(tab, win, wout, ids, facts):
     v = pltpu.VMEM
     return pl.pallas_call(
         front_kernel,
@@ -264,7 +262,7 @@
             jax.ShapeDtypeStruct((NY, 2, NX, 16, 2048), BF),
             jax.ShapeDtypeStruct((NY, 2, NX, 16, 512), BF),
         ),
-        in_specs=[VM] * 7,
+        in_specs=[VM] * 5,
         out_specs=(VM, VM, VM, ANY, ANY),
         scratch_shapes=[
             v((NZ, NY, 2, 128, COLS), BF),
@@ -281,7 +279,7 @@
         compiler_params=pltpu.CompilerParams(
             collective_id=0, has_side_effects=True, vmem_limit_bytes=VMEM_LIMIT
         ),
-    )(tab, win, wout, ids, lengths, surpluses, helpers)
+    )(tab, win, wout, ids, facts)
 
 
 def silu_grad(argument):
@@ -699,9 +697,7 @@
         weight_in.reshape(NX, 16, 2048),
         weight_out.reshape(NX, 16, 512),
         ids,
-        seq_lengths.reshape(NB, NSEQ),
-        surplus_slot,
-        helper_map,
+        jnp.concatenate([seq_lengths[:, 0, :], surplus_slot, helper_map], axis=1),
     )
     layer_out, table_sum, weight_sum = back(
         lengths, rows, cotangent[0], w_in.reshape(D, 4 * D), w_out.reshape(D, D), id_rows

time: 134 us -> 132 us (0.985)
  local copies, waits for them, and re-layouts: 4.74 us -> 2.97 us
    reshape x1 -> x0, local copies, waits for them, and re-layouts: 1.43 us -> none  [on_device(): seq_lengths.reshape(NB, NSEQ)]
where the time goes in v5:
time: 132 us; the launch traced here: 131 us
  Pallas kernels  126 us (95%)
  local copies, waits for them, and re-layouts  2.97 us (2%)
    pallas_call x1, Pallas kernels, back(): pl.pallas_call(back_kernel, name='back', out_shape=(jax.ShapeDtypeStruct(...  65.4 us
    pallas_call x1, Pallas kernels, front(): pl.pallas_call(front_kernel, name='front', out_shape=(jax.ShapeDtypeStruc...  58.9 us

profile of v5, /device:TPU:6, one launch (start us, length us, event | category | flops | bytes accessed | tf_op | source)
XLA Modules:
  0.0 130.7 jit_solution(15882315309059311353)
XLA Ops:
  0.6 0.0 copy-start
  0.7 0.8 copy.16
  1.5 0.7 copy.17
  2.2 0.7 copy.18
  3.0 0.7 pad_add_fusion.facts
  3.6 0.0 copy-done
  3.7 0.6 copy.21
  4.3 58.9 %front.1 = (bf16[256,512]{1,0:T(8,128)(2,1)}, s32[16,1024]{1,0:T(8,128)}, s32[8,128]{1,0:T(8,128)}, bf16[4,2,4,16,2048]{4,3,2,1,0:T(8,128)(2,1)}, bf16[4,2,4,16,512]{4,3,2,1,0:T(8,128)(2,1)}) custom-call(bf16[4,2,128,128]{3,2,1,0:T(8,128)(2,1)} %bitcast.22, bf16[4,16,2048]{2,1,0:T(8,128)(2,1)} %bitcast.23, bf16[4,16,512]{2,1,0:T(8,128)(2,1)} %bitcast.25, ...), custom_call_target="tpu_custom_call" | custom-call | tf_op jit(solution)/shard_map/front/pallas_call | solution.py:255
  63.2 65.4 %back.1 = (bf16[256,512]{1,0:T(8,128)(2,1)}, f32[128,128]{1,0:T(8,128)}, bf16[4,16,2560]{2,1,0:T(8,128)(2,1)}) custom-call(s32[8,128]{1,0:T(8,128)} %get-tuple-element.16.lengths, bf16[256,512]{1,0:T(8,128)(2,1)} %get-tuple-element.17.x_rows, bf16[256,512]{1,0:T(8,128)(2,1)} %bitcast.20, bf16[512,2048]{1,0:T(8,128)(2,1)} %bitcast.18, ...), custom_call_target="tpu_custom_call" | custom-call | tf_op jit(solution)/shard_map/back/pallas_call | solution.py:628
  128.6 2.0 %finish.1 = (bf16[256,512]{1,0:T(8,128)(2,1)}, f32[128,128]{1,0:T(8,128)}, f32[64,2048]{1,0:T(8,128)}, f32[64,512]{1,0:T(8,128)}) custom-call(bf16[256,512]{1,0:T(8,128)(2,1)} %get-tuple-element.21.layer_in, f32[128,128]{1,0:T(8,128)} %get-tuple-element.22.table_in, bf16[4,16,2560]{2,1,0:T(8,128)(2,1)} %get-tuple-element.23.we), custom_call_target="tpu_custom_call" | custom-call | tf_op jit(solution)/shard_map/finish/pallas_call | solution.py:675
  (2 shorter events, 0.0 us)
Async XLA Ops:
  0.6 3.0 %copy-start = (s32[1,16384,16]{1,2,0:T(8,128)S(1)}, s32[1,16384,16]{1,2,0:T(8,128)}, u32[]{:S(2)}) copy-start(s32[1,16384,16]{1,2,0:T(8,128)} %param.8) | copy-start | bytes 3145732
